TPU v7x, 32 devices: a whole 2x2x4 slice. The times are simulated.
32 devices in a mesh: context: 4 (over z), dp: 4 (over y, core), head: 2 (over x).
Axes of the slice: x: 2, y: 2, z: 4, core: 2. Of those that a mesh axis runs over, the one named last changes fastest.
Arguments:
- inputs: bfloat16 [4, 512, 2304], P('dp', 'context', 'head'), may hold values from -6 to 6
- output_grad: bfloat16 [4, 512, 2304], P('dp', 'context', 'head'), may hold values from -6 to 6
- qkv_weight: bfloat16 [2304, 3, 4096], P(None, None, 'head'), may hold values from -0.125 to 0.125
- out_weight: bfloat16 [2304, 4096], P(None, 'head'), may hold values from -0.09375 to 0.09375
- down_weight: bfloat16 [2304, 128], replicated, may hold values from -0.125 to 0.125
- up_weight: bfloat16 [128, 4096], P(None, 'head'), may hold values from -0.5 to 0.5
- beta_weight: bfloat16 [2304, 32], P(None, 'head'), may hold values from -0.125 to 0.125
- gate_bias: float32 [4096], P('head'), may hold values from -9 to -1.6, as said below
Outputs:
- layer_out: bfloat16 [4, 512, 2304], P('dp', 'context', 'head')
- input_grad: bfloat16 [4, 512, 2304], P('dp', 'context', 'head')
- qkv_grad: bfloat16 [2304, 3, 4096], P(('context', 'dp'), None, 'head')
- out_grad: bfloat16 [2304, 4096], P(('context', 'dp'), 'head')
- up_grad: float32 [128, 4096], P(None, 'head')
- down_grad: float32 [2304, 128], replicated
- beta_grad: float32 [2304, 32], P(None, 'head')
- bias_grad: float32 [4096], P('head')
Inputs may be any that keep to these rules, and one draw needn't show every extreme that they name: `gate_bias`: offsets of the decay gate, one per channel.
All inputs are finite; a program needn't handle non-finite values.
Results may differ from a plain program's by a relative error of at most 0.02.
Values may be sent and summed in bfloat16 or wider, within the bound.
A program may use at most 192 MiB of HBM per device.

v0:
```python
import jax
import jax.numpy as jnp
from jax import lax
from jax.sharding import PartitionSpec as P

SPAN = 64


epsilon = 1e-06
highest = lax.Precision.HIGHEST


def shifted(value, axis, by):
    count = lax.axis_size(axis)
    pairs = [(i, i + by) for i in range(count) if 0 <= i + by < count]
    return lax.ppermute(value, axis, pairs)


def product(pattern, left, right):
    return jnp.einsum(pattern, left, right, precision=highest)


def activate(projected, gate_pre, beta_logit):
    token_count = projected.shape[0]
    head_count = beta_logit.shape[1]
    head_width = projected.shape[2] // head_count
    blocks = projected.reshape(token_count, 3, head_count, head_width)

    def normalize(values):
        return values * lax.rsqrt(jnp.sum(values * values, axis=-1, keepdims=True) + epsilon)

    queries = jnp.swapaxes(normalize(blocks[:, 0]), 0, 1)
    key_rows = jnp.swapaxes(normalize(blocks[:, 1]), 0, 1)
    value_rows = jnp.swapaxes(blocks[:, 2], 0, 1)
    decays = jnp.swapaxes(
        (-0.25 * jax.nn.sigmoid(gate_pre)).reshape(token_count, head_count, head_width), 0, 1
    )
    betas = jnp.swapaxes(jax.nn.sigmoid(beta_logit), 0, 1)
    return (queries, key_rows, value_rows, decays, betas)


def span_terms(queries, key_rows, value_rows, decays, betas):
    leading = queries.shape[:-2]
    block_count = queries.shape[-2] // SPAN

    def blocked(member):
        return member.reshape(leading + (block_count, SPAN) + member.shape[-1:])

    queries, key_rows, value_rows, decays = (
        blocked(queries),
        blocked(key_rows),
        blocked(value_rows),
        blocked(decays),
    )
    betas = betas.reshape(leading + (block_count, SPAN))
    cumulative = jnp.cumsum(decays, axis=-2)
    middle = cumulative[..., SPAN // 2 - 1 : SPAN // 2, :]
    final_decay = cumulative[..., SPAN - 1 :, :]
    key_fwd = jnp.exp(cumulative - middle) * key_rows
    key_back = jnp.exp(middle - cumulative) * key_rows
    query_fwd = jnp.exp(cumulative - middle) * queries
    key_start = jnp.exp(cumulative) * key_rows
    query_start = jnp.exp(cumulative) * queries
    key_end = jnp.exp(final_decay - cumulative) * key_rows
    row_index = lax.broadcasted_iota(jnp.int32, (SPAN, SPAN), 0)
    col_index = lax.broadcasted_iota(jnp.int32, (SPAN, SPAN), 1)
    strict = (row_index > col_index).astype(jnp.float32)
    lower_mask = (row_index >= col_index).astype(jnp.float32)
    coupling = betas[..., :, None] * product("...tc,...sc->...ts", key_fwd, key_back) * strict
    powers = -coupling
    inverse = jnp.eye(SPAN, dtype=jnp.float32) + powers
    for section in range(1, (SPAN - 1).bit_length()):
        powers = product("...ts,...su->...tu", powers, powers)
        inverse = inverse + product("...ts,...su->...tu", inverse, powers)
    solver = inverse * betas[..., None, :]
    solved_values = product("...ts,...sc->...tc", solver, value_rows)
    solved_keys = product("...ts,...sc->...tc", solver, key_start)
    scores = product("...tc,...sc->...ts", query_fwd, key_back) * lower_mask
    query_eff = query_start - product("...ts,...sc->...tc", scores, solved_keys)
    local_out = product("...ts,...sc->...tc", scores, solved_values)
    side = queries.shape[-1]
    diagonal = jnp.eye(side, dtype=jnp.float32) * jnp.exp(final_decay)[..., 0, :, None]
    transition = diagonal - product("...sc,...sd->...cd", key_end, solved_keys)
    offset = product("...sc,...sd->...cd", key_end, solved_values)
    return (query_eff, local_out, transition, offset)


def chain(terms, state_in):

    def chain_advance(carried, pieces):
        query_eff, local_out, transition, offset = pieces
        emitted = product("...tc,...cd->...td", query_eff, carried) + local_out
        return (product("...cd,...de->...ce", transition, carried) + offset, emitted)

    moved = tuple((jnp.moveaxis(member, -3, 0) for member in terms))
    final_state, emitted = lax.scan(chain_advance, state_in, moved)
    return (jnp.moveaxis(emitted, 0, -3), final_state)


def compose_spans(transition, offset, identity):

    def compose_advance(carried, pieces):
        return (
            (
                product("hcd,hde->hce", pieces[0], carried[0]),
                product("hcd,hde->hce", pieces[0], carried[1]) + pieces[1],
            ),
            None,
        )

    moved = (jnp.moveaxis(transition, -3, 0), jnp.moveaxis(offset, -3, 0))
    combined, unused_rows = lax.scan(compose_advance, (identity, jnp.zeros_like(identity)), moved)
    return combined


def shards(
    inputs, output_grad, qkv_weight, out_weight, down_weight, up_weight, beta_weight, gate_bias
):
    gathered = lax.all_gather(inputs, "head", axis=2, tiled=True)[0]
    token_count, model_width = gathered.shape
    all_width = qkv_weight.shape[2]
    head_count = beta_weight.shape[1]
    head_width = all_width // head_count
    qkv_flat = qkv_weight.reshape(model_width, 3 * all_width)
    projected = jnp.dot(gathered, qkv_flat, preferred_element_type=jnp.float32).reshape(
        token_count, 3, all_width
    )
    low_rank = jnp.dot(gathered, down_weight, preferred_element_type=jnp.float32).astype(
        jnp.bfloat16
    )
    gate_pre = jnp.dot(low_rank, up_weight, preferred_element_type=jnp.float32) + gate_bias
    beta_logit = jnp.dot(gathered, beta_weight, preferred_element_type=jnp.float32)
    acts, act_vjp = jax.vjp(activate, projected, gate_pre, beta_logit)
    terms, terms_vjp = jax.vjp(span_terms, *acts)
    identity = jnp.broadcast_to(
        jnp.eye(head_width, dtype=jnp.float32), (head_count, head_width, head_width)
    )
    empty = jnp.zeros((head_count, head_width, head_width), jnp.float32)
    shard_linear, shard_offset = compose_spans(terms[2], terms[3], identity)

    def pass_state(position, incoming):
        leaving = product("hcd,hde->hce", shard_linear, incoming) + shard_offset
        return shifted(leaving.astype(jnp.bfloat16), "context", 1).astype(leaving.dtype)

    state_in = lax.fori_loop(0, lax.axis_size("context") - 1, pass_state, empty)
    (mixed_blocks, final_state), chain_vjp = jax.vjp(chain, terms, state_in)
    mixed = jnp.swapaxes(mixed_blocks.reshape(head_count, token_count, head_width), 0, 1)
    mixed = mixed.reshape(token_count, all_width).astype(jnp.bfloat16)
    out_part = jnp.einsum("tc,dc->td", mixed, out_weight, preferred_element_type=jnp.float32)
    layer_out = lax.psum_scatter(
        out_part.astype(jnp.bfloat16), "head", scatter_dimension=1, tiled=True
    )[None]
    grad_whole = lax.all_gather(output_grad, "head", axis=2, tiled=True)[0]
    mixed_grad = jnp.dot(grad_whole, out_weight, preferred_element_type=jnp.float32)
    grad_blocks = jnp.swapaxes(
        mixed_grad.reshape(token_count, head_count, head_width), 0, 1
    ).reshape(mixed_blocks.shape)
    own_grad = chain_vjp((grad_blocks, jnp.zeros_like(final_state)))[1]
    linear_back = jnp.swapaxes(shard_linear, 1, 2)

    def pass_grad(position, incoming):
        leaving = product("hcd,hde->hce", linear_back, incoming) + own_grad
        return shifted(leaving.astype(jnp.bfloat16), "context", -1).astype(leaving.dtype)

    state_grad = lax.fori_loop(0, lax.axis_size("context") - 1, pass_grad, empty)
    term_grads, unused_state = chain_vjp((grad_blocks, state_grad))
    proj_grad, pre_grad, logit_grad = act_vjp(terms_vjp(term_grads))
    proj_low = proj_grad.astype(jnp.bfloat16).reshape(token_count, 3 * all_width)
    gate_low = pre_grad.astype(jnp.bfloat16)
    logit_low = logit_grad.astype(jnp.bfloat16)
    low_grad = jnp.einsum(
        "tc,rc->tr", gate_low, up_weight, preferred_element_type=jnp.float32
    ).astype(jnp.bfloat16)
    input_part = jnp.einsum("tc,dc->td", proj_low, qkv_flat, preferred_element_type=jnp.float32)
    input_part = input_part + jnp.einsum(
        "tr,dr->td", low_grad, down_weight, preferred_element_type=jnp.float32
    )
    input_part = input_part + jnp.einsum(
        "th,dh->td", logit_low, beta_weight, preferred_element_type=jnp.float32
    )
    input_grad = lax.psum_scatter(
        input_part.astype(jnp.bfloat16), "head", scatter_dimension=1, tiled=True
    )[None]
    shard_rows = model_width // (lax.axis_size("context") * lax.axis_size("dp"))
    first = jnp.einsum("tr,tc->rc", gathered, proj_low, preferred_element_type=jnp.float32).reshape(
        lax.axis_size(("context", "dp")) * shard_rows, 3, all_width
    )
    second = jnp.einsum("tr,tc->rc", grad_whole, mixed, preferred_element_type=jnp.float32)
    summed = lax.psum_scatter(
        jnp.concatenate([first, second[:, None]], axis=1).astype(jnp.bfloat16),
        ("context", "dp"),
        scatter_dimension=0,
        tiled=True,
    ).astype(jnp.float32)
    qkv_grad = summed[:, :3].astype(jnp.bfloat16)
    out_grad = summed[:, 3].astype(jnp.bfloat16)
    up_term = jnp.einsum("tr,tc->rc", low_rank, gate_low, preferred_element_type=jnp.float32)
    beta_term = jnp.einsum("td,th->dh", gathered, logit_low, preferred_element_type=jnp.float32)
    bias_term = jnp.sum(pre_grad, axis=0)
    up_grad, beta_grad, bias_grad = (
        lax.psum(up_term.astype(jnp.bfloat16), ("context", "dp")).astype(jnp.float32),
        lax.psum(beta_term.astype(jnp.bfloat16), ("context", "dp")).astype(jnp.float32),
        lax.psum(bias_term.astype(jnp.bfloat16), ("context", "dp")).astype(jnp.float32),
    )
    down_term = jnp.einsum("td,tr->dr", gathered, low_grad, preferred_element_type=jnp.float32)
    down_grad = lax.psum(down_term, ("context", "dp", "head"))
    return (layer_out, input_grad, qkv_grad, out_grad, up_grad, down_grad, beta_grad, bias_grad)


def solution(mesh):
    return jax.shard_map(
        shards,
        mesh=mesh,
        in_specs=(
            P("dp", "context", "head"),
            P("dp", "context", "head"),
            P(None, None, "head"),
            P(None, "head"),
            P(),
            P(None, "head"),
            P(None, "head"),
            P("head"),
        ),
        out_specs=(
            P("dp", "context", "head"),
            P("dp", "context", "head"),
            P(("context", "dp"), None, "head"),
            P(("context", "dp"), "head"),
            P(None, "head"),
            P(),
            P(None, "head"),
            P("head"),
        ),
        check_vma=False,
    )
```

profile of v0, /device:TPU:0, one launch (start us, length us, event | category | flops | bytes accessed | tf_op | source)
XLA Modules:
  0.0 958.7 jit_solution(6293988146670006036)
XLA Ops:
  8.1 11.0 %all_gather.6 = bf16[1,128,2304]{2,1,0:T(8,128)(2,1)S(1)} all-gather(bf16[1,128,1152]{2,1,0:T(8,128)(2,1)} %param.20), channel_id=1, replica_groups=mesh['context'=4,'dp'=4,'head'=2] {'head'}, dimensions={2}, use_global_device_ids=true | all-gather | bytes 884736 | tf_op jit(solution)/shard_map/all_gather | solution.py:119
  23.5 36.8 %copy.144 = bf16[2304,3,2048]{0,2,1:T(8,128)(2,1)} copy(bf16[2304,3,2048]{2,0,1:T(8,128)(2,1)} %param.22) | data formatting | bytes 56623104 | tf_op args[2]
  60.3 15.5 %fusion.137 = f32[128,3,16,128]{3,0,2,1:T(8,128)} fusion(bf16[3,16,128,2304]{3,2,1,0:T(8,128)(2,1)} %bitcast.457, bf16[1,128,2304]{2,1,0:T(8,128)(2,1)S(1)} %all_gather.6), kind=kOutput, calls=%fused_computation.215 | convolution fusion | flops 3623878656 | bytes 32047104 | tf_op jit(solution)/shard_map/dot_general | solution.py:125
  89.1 3.1 fusion.165
  108.5 4.8 convolution_bitcast_fusion.4
  113.4 3.4 convolution_multiply_fusion
  119.0 2.9 fusion.89
  121.9 4.0 bitcast_subtract_fusion
  128.8 2.9 copy.161
  131.7 3.2 copy.150
  135.9 18.0 %while.88 = (s32[]{:T(128)}, f32[16,128,128]{2,1,0:T(8,128)}, f32[16,128,128]{2,1,0:T(8,128)}, f32[2,16,128,128]{3,2,1,0:T(8,128)}, f32[2,16,128,128]{3,2,1,0:T(8,128)}, /*index=5*/s32[]{:T(128)}, s32[]{:T(128)}) while((s32[]{:T(128)}, f32[16,128,128]{2,1,0:T(8,128)}, f32[16,128,128]{2,1,0:T(8,128)}, ...), condition=%wide.region_3.4_spmd.clone, body=%wide.region_2.0_spmd.clone.sunk | while | flops 805830656 | bytes 24118936 | solution.py:112
  141.3 3.7 convolution_add_fusion.37
  150.0 4.0 convolution_add_fusion.37
  158.9 56.0 %while.89 = (s32[]{:T(128)}, f32[16,128,128]{2,1,0:T(8,128)}, f32[16,128,128]{2,1,0:T(8,128)}, f32[16,128,128]{2,1,0:T(8,128)}, s32[]{:T(128)}, /*index=5*/s32[]{:T(128)}) while((s32[]{:T(128)}, f32[16,128,128]{2,1,0:T(8,128)}, f32[16,128,128]{2,1,0:T(8,128)}, f32[16,128,128]{2,1,0:T(8,128)}, s32[]{:T(128)}, ...), condition=%wide.region_5.6_spmd.clone, body=%wide.region_4.5_spmd.clone.sunk | while | flops 403701760 | bytes 7340151 | solution.py:145
  158.9 3.5 fusion.366
  162.4 3.7 collective-permute-start
  166.1 10.6 %collective-permute-done = bf16[16,128,128]{2,1,0:T(8,128)(2,1)S(1)} collective-permute-done((bf16[16,128,128]{2,1,0:T(8,128)(2,1)}, bf16[16,128,128]{2,1,0:T(8,128)(2,1)S(1)}, u32[]{:S(2)}, u32[]{:S(2)}) %collective-permute-start) | collective-permute-done | bytes 524320 | tf_op jit(solution)/shard_map/while/body/eval_jaxpr/ppermute | solution.py:16
  177.8 3.9 fusion.366
  181.6 4.3 collective-permute-start
  185.9 9.7 %collective-permute-done = bf16[16,128,128]{2,1,0:T(8,128)(2,1)S(1)} collective-permute-done((bf16[16,128,128]{2,1,0:T(8,128)(2,1)}, bf16[16,128,128]{2,1,0:T(8,128)(2,1)S(1)}, u32[]{:S(2)}, u32[]{:S(2)}) %collective-permute-start) | collective-permute-done | bytes 524320 | tf_op jit(solution)/shard_map/while/body/eval_jaxpr/ppermute | solution.py:16
  196.7 3.9 fusion.366
  200.6 4.3 collective-permute-start
  204.9 8.9 collective-permute-done
  216.4 12.5 %while.86 = (s32[]{:T(128)}, f32[16,128,128]{2,1,0:T(8,128)}, bf16[2,16,64,128]{3,2,0,1:T(8,128)(2,1)S(1)}, f32[2,16,128,128]{3,2,1,0:T(8,128)}, f32[2,16,128,12...) while((s32[]{:T(128)}, f32[16,128,128]{2,1,0:T(8,128)}, ...), condition=%wide.region_8.9_spmd, body=%wide.region_7.8_spmd.sunk | while | flops 604372992 | bytes 36178136 | solution.py:96
  229.0 13.0 %copy.236 = bf16[2048,2304]{1,0:T(8,128)(2,1)} copy(bf16[2048,2304]{0,1:T(8,128)(2,1)} %bitcast.458) | data formatting | bytes 18874368 | tf_op jit(solution)/shard_map/dot_general | solution.py:154
  241.9 7.6 all_gather.7
  249.5 5.8 fusion.139
  256.4 11.1 %while.90 = (s32[]{:T(128)}, f32[16,128,128]{2,1,0:T(8,128)}, f32[2,16,128,128]{2,3,1,0:T(8,128)}, f32[2,16,64,128]{3,2,1,0:T(8,128)}, f32[2,16,64,128]{3,2,1,0:T(8,128)}, /*index=5*/s32[]{:T(128)}, s32[]{:T(128)}) while((s32[]{:T(128)}, f32[16,128,128]{2,1,0:T(8,128)}, f32[2,16,128,128]{2,3,1,0:T(8,128)}, ...), condition=%wide.region_11.12_spmd.clone, body=%wide.region_10.11_spmd.clone.sunk | while | flops 604504064 | bytes 14681255 | solution.py:96
  259.0 2.8 convolution_add_fusion.38
  261.8 2.8 fusion.371
  264.7 2.8 convolution_add_fusion.38
  267.5 45.2 %while.91 = (s32[]{:T(128)}, f32[16,128,128]{2,1,0:T(8,128)S(1)}, f32[16,128,128]{2,1,0:T(8,128)}, f32[16,128,128]{2,1,0:T(8,128)}, s32[]{:T(128)}, /*index=5*/s32[]{:T(128)}) while((s32[]{:T(128)}, f32[16,128,128]{2,1,0:T(8,128)S(1)}, f32[16,128,128]{2,1,0:T(8,128)}, f32[16,128,128]{2,1,0:T(8,128)}, s32[]{:T(128)}, ...), condition=%wide.region_13.14_spmd.clone, body=%wide.region_12.13_spmd.clone.sunk | while | flops 403701760 | bytes 7340151 | solution.py:165
  267.5 3.5 fusion.374
  272.3 10.5 %collective-permute-done.1 = bf16[16,128,128]{2,1,0:T(8,128)(2,1)S(1)} collective-permute-done((bf16[16,128,128]{2,1,0:T(8,128)(2,1)}, bf16[16,128,128]{2,1,0:T(8,128)(2,1)S(1)}, u32[]{:S(2)}, u32[]{:S(2)}) %collective-permute-start.1) | collective-permute-done | bytes 524320 | tf_op jit(solution)/shard_map/while/body/eval_jaxpr/ppermute | solution.py:16
  283.0 3.5 fusion.374
  287.8 10.0 %collective-permute-done.1 = bf16[16,128,128]{2,1,0:T(8,128)(2,1)S(1)} collective-permute-done((bf16[16,128,128]{2,1,0:T(8,128)(2,1)}, bf16[16,128,128]{2,1,0:T(8,128)(2,1)S(1)}, u32[]{:S(2)}, u32[]{:S(2)}) %collective-permute-start.1) | collective-permute-done | bytes 524320 | tf_op jit(solution)/shard_map/while/body/eval_jaxpr/ppermute | solution.py:16
  297.9 3.5 fusion.374
  302.7 10.0 %collective-permute-done.1 = bf16[16,128,128]{2,1,0:T(8,128)(2,1)S(1)} collective-permute-done((bf16[16,128,128]{2,1,0:T(8,128)(2,1)}, bf16[16,128,128]{2,1,0:T(8,128)(2,1)S(1)}, u32[]{:S(2)}, u32[]{:S(2)}) %collective-permute-start.1) | collective-permute-done | bytes 524320 | tf_op jit(solution)/shard_map/while/body/eval_jaxpr/ppermute | solution.py:16
  318.1 24.5 %while.87 = (s32[]{:T(128)}, f32[16,128,128]{2,1,0:T(8,128)S(1)}, f32[2,16,64,128]{3,2,0,1:T(8,128)}, f32[2,16,64,128]{3,2,1,0:T(8,128)}, f32[2,16,128,128]{2,3,...) while((s32[]{:T(128)}, f32[16,128,128]{2,1,0:T(8,128)S(1)}, ...), condition=%wide.region_15.16_spmd, body=%wide.region_14.15_spmd.sunk | while | flops 1208221696 | bytes 56627052 | solution.py:96
  320.1 3.3 fusion.358
  332.2 3.3 fusion.358
  342.7 3.5 fusion.112
  346.3 4.2 fusion.85
  392.1 2.9 fusion.172
  395.0 3.2 fusion.173
  398.2 3.2 fusion.70
  405.1 2.8 fusion.189
  407.9 3.5 fusion.167
  411.3 3.1 copy.199
  414.4 4.8 multiply_reduce_fusion.1
  421.4 4.2 fusion.82
  427.1 4.3 fusion.156
  432.4 4.6 fusion.107
  444.5 7.9 convolution_convert_fusion.2
  464.7 14.7 %convolution_bitcast_fusion.3 = f32[128,2304]{1,0:T(8,128)S(1)} fusion(bf16[128,3,2048]{0,2,1:T(8,128)(2,1)} %bitcast.465, bf16[2304,3,2048]{2,0,1:T(8,128)(2,1)} %param.22), kind=kOutput, calls=%fused_computation.80 | convolution fusion | flops 3623878656 | bytes 31064064 | tf_op jit(solution)/shard_map/tc,dc->td/dot_general | solution.py:174
  481.9 5.1 fusion.61
  486.9 12.8 %copy.205 = bf16[2304,1,2048]{2,0,1:T(8,128)(2,1)} copy(bf16[2304,1,2048]{0,2,1:T(8,128)(2,1)} %fusion.61) | data formatting | bytes 18874368 | tf_op jit(solution)/shard_map/broadcast_in_dim | solution.py:190
  499.7 14.2 %convolution_convert_fusion = bf16[6144,2304]{1,0:T(8,128)(2,1)} fusion(bf16[128,6144]{0,1:T(8,128)(2,1)} %bitcast.466, bf16[1,128,2304]{2,1,0:T(8,128)(2,1)S(1)} %copy-done.34), kind=kOutput, calls=%fused_computation.74 | convolution fusion | flops 3638034432 | bytes 30474240 | tf_op jit(solution)/shard_map/tr,tc->rc/dot_general | solution.py:185
  513.9 36.6 %copy.204 = bf16[2304,3,2048]{2,0,1:T(8,128)(2,1)} copy(bf16[2304,3,2048]{0,2,1:T(8,128)(2,1)} %bitcast.455) | data formatting | bytes 56623104 | tf_op jit(solution)/shard_map/reshape | solution.py:185
  550.5 26.2 %pad_maximum_fusion = bf16[2304,4,2048]{2,0,1:T(8,128)(2,1)} fusion(bf16[2304,1,2048]{2,0,1:T(8,128)(2,1)} %copy.205, bf16[2304,3,2048]{2,0,1:T(8,128)(2,1)} %copy.204), kind=kLoop, calls=%fused_computation.73 | loop fusion | flops 18874368 | bytes 75497472 | tf_op jit(solution)/shard_map/concatenate | solution.py:190
  576.7 29.5 %psum.31 = bf16[2048]{0:T(1024)(128)(2,1)S(1)} all-reduce(bf16[2048]{0:T(1024)(128)(2,1)S(1)} %get-tuple-element.701), channel_id=1, replica_groups=mesh['context'=4,'dp'=4,'head'=2] {'context','dp'}, use_global_device_ids=true, to_apply=%region_32.33 | all-reduce | flops 2048 | bytes 8192 | tf_op jit(solution)/shard_map/psum | solution.py:203
  610.6 131.2 %all-reduce.9.cloned.1.call-done = f32[2304,128]{0,1:T(8,128)} async-done(((f32[2304,128]{0,1:T(8,128)}), f32[2304,128]{0,1:T(8,128)}) %all-reduce.9.cloned.1.call-update) | async-done | bytes 1179664 | tf_op jit(solution)/shard_map/psum | solution.py:206
  748.2 197.9 %reduce-scatter.8.cloned.1.call-done = bf16[144,4,2048]{2,0,1:T(8,128)(2,1)} async-done(((bf16[2304,4,2048]{2,0,1:T(8,128)(2,1)}), bf16[144,4,2048]{2,0,1:T(8,128)(2,1)}) %reduce-scatter.8.cloned.1.call-update) | async-done | bytes 2359312 | tf_op jit(solution)/shard_map/reduce_scatter | solution.py:189
  946.1 2.9 slice.35
  (391 shorter events, 186.4 us)
Async XLA Ops:
  8.0 11.2 %copy-start = (bf16[2304,128]{1,0:T(8,128)(2,1)S(1)}, bf16[2304,128]{1,0:T(8,128)(2,1)}, u32[]{:S(2)}) copy-start(bf16[2304,128]{1,0:T(8,128)(2,1)} %param.24) | copy-start | bytes 1769476
  8.0 11.5 %copy-start.87 = (bf16[128,2048]{1,0:T(8,128)(2,1)S(1)}, bf16[128,2048]{1,0:T(8,128)(2,1)}, u32[]{:S(2)}) copy-start(bf16[128,2048]{1,0:T(8,128)(2,1)} %param.25) | copy-start | bytes 1572868
  8.0 11.5 %copy-start.103 = (f32[2048]{0:T(1024)S(1)}, f32[2048]{0:T(1024)}, u32[]{:S(2)}) copy-start(f32[2048]{0:T(1024)} %param.27) | copy-start | bytes 24580
  8.0 598.8 %all-reduce.11.cloned.1.call-start = ((), (), s32[]{:S(2)}) async-start(), calls=%async_computation.7 | async-start | bytes 1196032 | tf_op jit(solution)/shard_map/psum | solution.py:201
  19.2 65.0 %copy-start.33 = (bf16[1,128,2304]{2,1,0:T(8,128)(2,1)}, bf16[1,128,2304]{2,1,0:T(8,128)(2,1)S(1)}, u32[]{:S(2)}) copy-start(bf16[1,128,2304]{2,1,0:T(8,128)(2,1)S(1)} %all_gather.6) | copy-start | bytes 1769476
  75.8 8.4 copy-start.89
  78.0 7.1 copy-start.98
  78.1 7.1 copy-start.100
  82.8 5.4 copy-start.94
  88.3 25.1 %copy-start.3 = (f32[128,16,128]{2,0,1:T(8,128)}, f32[128,16,128]{2,0,1:T(8,128)S(1)}, u32[]{:S(2)}) copy-start(f32[128,16,128]{2,0,1:T(8,128)S(1)} %get-tuple-element.700) | copy-start | bytes 3145732
  88.3 30.7 %copy-start.29 = (f32[128,16,128]{2,0,1:T(8,128)}, f32[128,16,128]{2,0,1:T(8,128)S(1)}, u32[]{:S(2)}) copy-start(f32[128,16,128]{2,0,1:T(8,128)S(1)} %get-tuple-element.699) | copy-start | bytes 3145732
  89.1 32.9 %copy-start.40 = (f32[16,2,64,128]{3,2,1,0:T(8,128)}, f32[16,2,64,128]{3,2,1,0:T(8,128)S(1)}, u32[]{:S(2)}) copy-start(f32[16,2,64,128]{3,2,1,0:T(8,128)S(1)} %fusion.135) | copy-start | bytes 3145732
  92.2 2.7 copy-start.14
  94.9 2.7 copy-start.16
  96.4 2.5 copy-start.63
  97.6 2.5 copy-start.18
  100.1 2.6 copy-start.20
  101.5 2.5 copy-start.67
  102.8 2.6 copy-start.52
  104.1 3.2 copy-start.54
  107.2 14.7 %copy-start.42 = (f32[16,2,64,128]{3,2,1,0:T(8,128)}, f32[16,2,64,128]{3,2,1,0:T(8,128)S(1)}, u32[]{:S(2)}) copy-start(f32[16,2,64,128]{3,2,1,0:T(8,128)S(1)} %fusion.133) | copy-start | bytes 3145732
  108.5 8.2 copy-start.35
  116.8 5.2 copy-start.38
  119.0 2.9 copy-start.102
  137.7 2.6 copy-start.7
  146.4 2.7 copy-start.7
  162.4 14.3 %collective-permute-start = (bf16[16,128,128]{2,1,0:T(8,128)(2,1)}, bf16[16,128,128]{2,1,0:T(8,128)(2,1)S(1)}, u32[]{:S(2)}, u32[]{:S(2)}) collective-permute-start(bf16[16,128,128]{2,1,0:T(8,128)(2,1)} %fusion.366), channel_id=1, source_target_pairs={{0,8},{8,16},{16,24},{1,9},{9,17},{17,25},{2,10},{10,18},{18,26},{... | collective-permute-start | bytes 1572872 | tf_op jit(solution)/shard_map/while/body/eval_jaxpr/ppermute | solution.py:16
  181.6 14.0 %collective-permute-start = (bf16[16,128,128]{2,1,0:T(8,128)(2,1)}, bf16[16,128,128]{2,1,0:T(8,128)(2,1)S(1)}, u32[]{:S(2)}, u32[]{:S(2)}) collective-permute-start(bf16[16,128,128]{2,1,0:T(8,128)(2,1)} %fusion.366), channel_id=1, source_target_pairs={{0,8},{8,16},{16,24},{1,9},{9,17},{17,25},{2,10},{10,18},{18,26},{... | collective-permute-start | bytes 1572872 | tf_op jit(solution)/shard_map/while/body/eval_jaxpr/ppermute | solution.py:16
  200.6 13.2 %collective-permute-start = (bf16[16,128,128]{2,1,0:T(8,128)(2,1)}, bf16[16,128,128]{2,1,0:T(8,128)(2,1)S(1)}, u32[]{:S(2)}, u32[]{:S(2)}) collective-permute-start(bf16[16,128,128]{2,1,0:T(8,128)(2,1)} %fusion.366), channel_id=1, source_target_pairs={{0,8},{8,16},{16,24},{1,9},{9,17},{17,25},{2,10},{10,18},{18,26},{... | collective-permute-start | bytes 1572872 | tf_op jit(solution)/shard_map/while/body/eval_jaxpr/ppermute | solution.py:16
  216.4 2.5 copy-start.8
  216.4 2.5 copy-start.51
  217.8 2.7 copy-start.11
  224.1 2.7 copy-start.11
  229.0 13.0 %copy-start.85 = (bf16[2,16,64,128]{3,2,0,1:T(8,128)(2,1)}, bf16[2,16,64,128]{3,2,0,1:T(8,128)(2,1)S(1)}, u32[]{:S(2)}) copy-start(bf16[2,16,64,128]{3,2,0,1:T(8,128)(2,1)S(1)} %get-tuple-element.430) | copy-start | bytes 1572868
  249.5 5.8 copy-start.78
  256.4 2.5 copy-start.5
  256.5 2.5 copy-start.9
  261.8 2.8 copy-start.5
  261.8 2.9 copy-start.9
  271.0 11.8 %collective-permute-start.1 = (bf16[16,128,128]{2,1,0:T(8,128)(2,1)}, bf16[16,128,128]{2,1,0:T(8,128)(2,1)S(1)}, u32[]{:S(2)}, u32[]{:S(2)}) collective-permute-start(bf16[16,128,128]{2,1,0:T(8,128)(2,1)} %fusion.374), channel_id=1, source_target_pairs={{8,0},{16,8},{24,16},{9,1},{17,9},{25,17},{10,2},{18,10},{26,18},{... | collective-permute-start | bytes 1572872 | tf_op jit(solution)/shard_map/while/body/eval_jaxpr/ppermute | solution.py:16
  286.5 11.3 %collective-permute-start.1 = (bf16[16,128,128]{2,1,0:T(8,128)(2,1)}, bf16[16,128,128]{2,1,0:T(8,128)(2,1)S(1)}, u32[]{:S(2)}, u32[]{:S(2)}) collective-permute-start(bf16[16,128,128]{2,1,0:T(8,128)(2,1)} %fusion.374), channel_id=1, source_target_pairs={{8,0},{16,8},{24,16},{9,1},{17,9},{25,17},{10,2},{18,10},{26,18},{... | collective-permute-start | bytes 1572872 | tf_op jit(solution)/shard_map/while/body/eval_jaxpr/ppermute | solution.py:16
  301.4 11.3 %collective-permute-start.1 = (bf16[16,128,128]{2,1,0:T(8,128)(2,1)}, bf16[16,128,128]{2,1,0:T(8,128)(2,1)S(1)}, u32[]{:S(2)}, u32[]{:S(2)}) collective-permute-start(bf16[16,128,128]{2,1,0:T(8,128)(2,1)} %fusion.374), channel_id=1, source_target_pairs={{8,0},{16,8},{24,16},{9,1},{17,9},{25,17},{10,2},{18,10},{26,18},{... | collective-permute-start | bytes 1572872 | tf_op jit(solution)/shard_map/while/body/eval_jaxpr/ppermute | solution.py:16
  319.2 4.2 copy-start.12
  324.9 4.0 copy-start.60
  331.3 4.2 copy-start.12
  337.0 4.0 copy-start.60
  342.7 3.6 copy-start.32
  342.7 3.6 copy-start.41
  346.3 4.2 copy-start.4
  350.5 2.5 copy-start.39
  383.8 6.1 copy-start.69
  395.0 3.2 copy-start.43
  398.2 3.2 copy-start.36
  405.0 2.8 copy-start.30
  421.4 4.2 copy-start.75
  421.4 4.9 copy-start.83
  427.1 5.3 copy-start.27
  427.1 5.3 copy-start.50
  427.1 5.3 copy-start.71
  441.6 300.3 %all-reduce.9.cloned.1.call-start = ((), (), s32[]{:S(2)}) async-start(), calls=%async_computation.4 | async-start | bytes 2359296 | tf_op jit(solution)/shard_map/psum | solution.py:206
  443.3 301.2 %reduce-scatter.10.cloned.1.call-start = ((), (), s32[]{:S(2)}) async-start(), calls=%async_computation.5 | async-start | bytes 884736
  444.5 10.2 %copy-start.57 = (f32[16,2,64,128]{3,2,1,0:T(8,128)S(1)}, f32[16,2,64,128]{3,2,1,0:T(8,128)}, u32[]{:S(2)}) copy-start(f32[16,2,64,128]{3,2,1,0:T(8,128)} %copy-done.56) | copy-start | bytes 3145732
  454.6 291.7 %reduce-scatter.12.cloned.1.call-start = ((), (), s32[]{:S(2)}) async-start(), calls=%async_computation.6 | async-start | bytes 884736
  481.8 464.3 %reduce-scatter.8.cloned.1.call-start = ((), (), s32[]{:S(2)}) async-start(), calls=%async_computation.3 | async-start | bytes 40108032 | tf_op jit(solution)/shard_map/reduce_scatter | solution.py:189
  (67 other events, 121.0 us)
Sparse Core Ops, SparseCore 0:
  441.7 91.3 all-reduce.10
  539.0 202.7 all-reduce.8
Sparse Core Ops, SparseCore 1:
  454.7 15.8 reduce-scatter.9
  481.9 15.8 reduce-scatter.11
  576.8 369.3 reduce-scatter.7
where the time goes:
time: 967 us; the launch traced here: 959 us
  waiting for transfers between devices  389 us (40%)
  matrix products  263 us (27%)
  local copies, waits for them, and re-layouts  174 us (18%)
  other arithmetic  49.9 us (5%)
  blocking collectives  48.2 us (5%)
  between operations  17.4 us (2%)
  starting transfers between devices  16.3 us (2%)
    reduce_scatter x1, waiting for transfers between devices, shards(): lax.psum_scatter(jnp.concatenate([first, second[:, None]], axis=1).astype...  198 us
    dot_general x80, matrix products, product(): return jnp.einsum(pattern, left, right, precision=highest)  194 us
    psum x1, waiting for transfers between devices, shards(): down_grad = lax.psum(down_term, ('context', 'dp', 'head'))  131 us
    ppermute x6, waiting for transfers between devices, shifted(): return lax.ppermute(value, axis, pairs)  59.7 us
    unnamed x186, local copies, waits for them, and re-layouts  59.4 us
    reshape x1, local copies, waits for them, and re-layouts, shards(): jnp.einsum('tr,tc->rc', gathered, proj_low, preferred_element_type=jnp.fl...  36.6 us
    psum x1, blocking collectives, shards(): lax.psum(bias_term.astype(jnp.bfloat16), ('context', 'dp'))  29.5 us
    concatenate x1, other arithmetic, shards(): jnp.concatenate([first, second[:, None]], axis=1).astype(jnp.bfloat16)  26.2 us
  transfers between devices with their start and end apart: 11, of which 8 were waited for; matrix products, arithmetic and copies ran while one was open for 15% of the time, Pallas kernels for 0%

commit v1 on v0

--- a/solution.py
+++ b/solution.py
@@ -7,7 +7,7 @@
 
 
 epsilon = 1e-06
-highest = lax.Precision.HIGHEST
+highest = lax.Precision.HIGH
 
 
 def shifted(value, axis, by):
@@ -138,72 +138,89 @@
     empty = jnp.zeros((head_count, head_width, head_width), jnp.float32)
     shard_linear, shard_offset = compose_spans(terms[2], terms[3], identity)
 
-    def pass_state(position, incoming):
-        leaving = product("hcd,hde->hce", shard_linear, incoming) + shard_offset
-        return shifted(leaving.astype(jnp.bfloat16), "context", 1).astype(leaving.dtype)
-
-    state_in = lax.fori_loop(0, lax.axis_size("context") - 1, pass_state, empty)
+    grad_whole = lax.all_gather(output_grad, "head", axis=2, tiled=True)[0]
+    mixed_grad = jnp.dot(grad_whole, out_weight, preferred_element_type=jnp.float32)
+    grad_blocks = jnp.swapaxes(
+        mixed_grad.reshape(token_count, head_count, head_width), 0, 1
+    ).reshape(terms[1].shape)
+    own_grad = jnp.zeros_like(empty)
+    for block in reversed(range(token_count // SPAN)):
+        own_grad = product("hcd,hce->hde", terms[2][:, block], own_grad) + product(
+            "htc,htd->hcd", terms[0][:, block], grad_blocks[:, block]
+        )
+    linear_back = jnp.swapaxes(shard_linear, 1, 2)
+    shard_count = lax.axis_size("context")
+    shard_index = lax.axis_index("context")
+    state_in, state_grad = empty, empty
+    for step in range(shard_count - 1):
+        leaving = shard_offset
+        leaving_grad = own_grad
+        if step:
+            leaving = product("hcd,hde->hce", shard_linear, state_in) + leaving
+            leaving_grad = product("hcd,hde->hce", linear_back, state_grad) + leaving_grad
+        state_in = shifted(leaving.astype(jnp.bfloat16), "context", 1).astype(jnp.float32)
+        state_grad = shifted(leaving_grad.astype(jnp.bfloat16), "context", -1).astype(jnp.float32)
     (mixed_blocks, final_state), chain_vjp = jax.vjp(chain, terms, state_in)
     mixed = jnp.swapaxes(mixed_blocks.reshape(head_count, token_count, head_width), 0, 1)
     mixed = mixed.reshape(token_count, all_width).astype(jnp.bfloat16)
+    slab = model_width // shard_count
+
+    def slab_of(member):
+        whole = lax.all_gather(member, "context", axis=0, tiled=True)
+        return lax.dynamic_slice_in_dim(whole, shard_index * slab, slab, axis=1)
+
+    def weight_term(rows, columns):
+        whole = lax.all_gather(columns, "context", axis=0, tiled=True)
+        term = jnp.einsum("tr,tc->rc", rows, whole, preferred_element_type=jnp.float32)
+        return lax.psum_scatter(
+            term.astype(jnp.bfloat16), "dp", scatter_dimension=0, tiled=True
+        )
+
+    input_slab = slab_of(gathered)
+    grad_slab = slab_of(grad_whole)
+    out_grad = weight_term(grad_slab, mixed)
     out_part = jnp.einsum("tc,dc->td", mixed, out_weight, preferred_element_type=jnp.float32)
     layer_out = lax.psum_scatter(
         out_part.astype(jnp.bfloat16), "head", scatter_dimension=1, tiled=True
     )[None]
-    grad_whole = lax.all_gather(output_grad, "head", axis=2, tiled=True)[0]
-    mixed_grad = jnp.dot(grad_whole, out_weight, preferred_element_type=jnp.float32)
-    grad_blocks = jnp.swapaxes(
-        mixed_grad.reshape(token_count, head_count, head_width), 0, 1
-    ).reshape(mixed_blocks.shape)
-    own_grad = chain_vjp((grad_blocks, jnp.zeros_like(final_state)))[1]
-    linear_back = jnp.swapaxes(shard_linear, 1, 2)
-
-    def pass_grad(position, incoming):
-        leaving = product("hcd,hde->hce", linear_back, incoming) + own_grad
-        return shifted(leaving.astype(jnp.bfloat16), "context", -1).astype(leaving.dtype)
-
-    state_grad = lax.fori_loop(0, lax.axis_size("context") - 1, pass_grad, empty)
     term_grads, unused_state = chain_vjp((grad_blocks, state_grad))
     proj_grad, pre_grad, logit_grad = act_vjp(terms_vjp(term_grads))
-    proj_low = proj_grad.astype(jnp.bfloat16).reshape(token_count, 3 * all_width)
+    proj_parts = [proj_grad[:, part].astype(jnp.bfloat16) for part in range(3)]
+    qkv_grad = jnp.stack([weight_term(input_slab, part) for part in proj_parts], axis=1)
     gate_low = pre_grad.astype(jnp.bfloat16)
     logit_low = logit_grad.astype(jnp.bfloat16)
     low_grad = jnp.einsum(
         "tc,rc->tr", gate_low, up_weight, preferred_element_type=jnp.float32
     ).astype(jnp.bfloat16)
-    input_part = jnp.einsum("tc,dc->td", proj_low, qkv_flat, preferred_element_type=jnp.float32)
-    input_part = input_part + jnp.einsum(
+    up_term = jnp.einsum("tr,tc->rc", low_rank, gate_low, preferred_element_type=jnp.float32)
+    beta_term = jnp.einsum("td,th->dh", gathered, logit_low, preferred_element_type=jnp.float32)
+    bias_term = jnp.sum(pre_grad, axis=0)
+    down_term = jnp.einsum("td,tr->dr", gathered, low_grad, preferred_element_type=jnp.float32)
+    small = [up_term, down_term, beta_term, bias_term]
+    packed = jnp.concatenate([term.astype(jnp.bfloat16).reshape(-1, 128) for term in small], axis=0)
+    packed = lax.psum(packed, ("context", "dp")).astype(jnp.float32)
+    results, start = [], 0
+    for term in small:
+        count = term.size // 128
+        results.append(packed[start : start + count].reshape(term.shape))
+        start += count
+    up_grad, down_grad, beta_grad, bias_grad = results
+    down_grad = lax.psum(down_grad, "head")
+    input_part = jnp.einsum(
         "tr,dr->td", low_grad, down_weight, preferred_element_type=jnp.float32
     )
     input_part = input_part + jnp.einsum(
         "th,dh->td", logit_low, beta_weight, preferred_element_type=jnp.float32
+    )
+    input_part = input_part + jnp.einsum(
+        "tc,dc->td",
+        jnp.concatenate(proj_parts, axis=1),
+        qkv_flat,
+        preferred_element_type=jnp.float32,
     )
     input_grad = lax.psum_scatter(
         input_part.astype(jnp.bfloat16), "head", scatter_dimension=1, tiled=True
     )[None]
-    shard_rows = model_width // (lax.axis_size("context") * lax.axis_size("dp"))
-    first = jnp.einsum("tr,tc->rc", gathered, proj_low, preferred_element_type=jnp.float32).reshape(
-        lax.axis_size(("context", "dp")) * shard_rows, 3, all_width
-    )
-    second = jnp.einsum("tr,tc->rc", grad_whole, mixed, preferred_element_type=jnp.float32)
-    summed = lax.psum_scatter(
-        jnp.concatenate([first, second[:, None]], axis=1).astype(jnp.bfloat16),
-        ("context", "dp"),
-        scatter_dimension=0,
-        tiled=True,
-    ).astype(jnp.float32)
-    qkv_grad = summed[:, :3].astype(jnp.bfloat16)
-    out_grad = summed[:, 3].astype(jnp.bfloat16)
-    up_term = jnp.einsum("tr,tc->rc", low_rank, gate_low, preferred_element_type=jnp.float32)
-    beta_term = jnp.einsum("td,th->dh", gathered, logit_low, preferred_element_type=jnp.float32)
-    bias_term = jnp.sum(pre_grad, axis=0)
-    up_grad, beta_grad, bias_grad = (
-        lax.psum(up_term.astype(jnp.bfloat16), ("context", "dp")).astype(jnp.float32),
-        lax.psum(beta_term.astype(jnp.bfloat16), ("context", "dp")).astype(jnp.float32),
-        lax.psum(bias_term.astype(jnp.bfloat16), ("context", "dp")).astype(jnp.float32),
-    )
-    down_term = jnp.einsum("td,tr->dr", gathered, low_grad, preferred_element_type=jnp.float32)
-    down_grad = lax.psum(down_term, ("context", "dp", "head"))
     return (layer_out, input_grad, qkv_grad, out_grad, up_grad, down_grad, beta_grad, bias_grad)
 
 

time: 967 us -> 768 us (0.79)
  matrix products: 263 us -> 184 us
  local copies, waits for them, and re-layouts: 174 us -> 132 us
  blocking collectives: 48.2 us -> 19.4 us
  other arithmetic: 49.9 us -> 22.7 us
  waiting for transfers between devices: 389 us -> 365 us
    reduce_scatter x1 -> x4, waiting for transfers between devices: 198 us -> 113 us  [weight_term(): lax.psum_scatter(term.astype(jnp.bfloat16), 'dp', scatter_dimension=0, ti...]
    dot_general x80 -> x78, matrix products: 194 us -> 120 us  [product(): return jnp.einsum(pattern, left, right, precision=highest)]
    all_gather x0 -> x6, waiting for transfers between devices: none -> 68.5 us  [the longest x4 47.1 us: weight_term(): whole = lax.all_gather(columns, 'context', axis=0, tiled=True)]
    ppermute x6, waiting for transfers between devices: 59.7 us -> 5.3 us  [shifted(): return lax.ppermute(value, axis, pairs)]
    psum x2, waiting for transfers between devices: 131 us -> 175 us  [the longest x1 175 us: shards(): packed = lax.psum(packed, ('context', 'dp')).astype(jnp.float32)]
    reshape x1 -> x6, local copies, waits for them, and re-layouts: 36.6 us -> 3.25 us  [the longest x4 1.77 us: shards(): term.astype(jnp.bfloat16).reshape(-1, 128)]
    psum x1 -> x0, blocking collectives: 29.5 us -> none  [shards(): lax.psum(bias_term.astype(jnp.bfloat16), ('context', 'dp'))]
    concatenate x1 -> x0, other arithmetic: 26.2 us -> none  [shards(): jnp.concatenate([first, second[:, None]], axis=1).astype(jnp.bfloat16)]
  transfers between devices with their start and end apart: 11 -> 20, of which waited for: 8 -> 10; matrix products, arithmetic and copies ran while one was open for 15% -> 16% of each run, Pallas kernels for 0% -> 0%
where the time goes in v1:
time: 768 us; the launch traced here: 760 us
  waiting for transfers between devices  365 us (48%)
  matrix products  184 us (24%)
  local copies, waits for them, and re-layouts  132 us (17%)
  other arithmetic  22.7 us (3%)
  blocking collectives  19.4 us (3%)
  starting transfers between devices  19.1 us (2%)
  between operations  17.6 us (2%)
    psum x1, waiting for transfers between devices, shards(): packed = lax.psum(packed, ('context', 'dp')).astype(jnp.float32)  175 us
    dot_general x78, matrix products, product(): return jnp.einsum(pattern, left, right, precision=highest)  120 us
    reduce_scatter x4, waiting for transfers between devices, weight_term(): lax.psum_scatter(term.astype(jnp.bfloat16), 'dp', scatter_dimension=0, ti...  113 us
    unnamed x192, local copies, waits for them, and re-layouts  65.9 us
    all_gather x4, waiting for transfers between devices, weight_term(): whole = lax.all_gather(columns, 'context', axis=0, tiled=True)  47.1 us
    all_gather x2, waiting for transfers between devices, slab_of(): whole = lax.all_gather(member, 'context', axis=0, tiled=True)  21.4 us
    dot_general x4, matrix products, weight_term(): jnp.einsum('tr,tc->rc', rows, whole, preferred_element_type=jnp.float32)  20.5 us
    ppermute x6, starting transfers between devices, shifted(): return lax.ppermute(value, axis, pairs)  18.2 us
  transfers between devices with their start and end apart: 20, of which 10 were waited for; matrix products, arithmetic and copies ran while one was open for 16% of the time, Pallas kernels for 0%

profile of v1, /device:TPU:0, one launch (start us, length us, event | category | flops | bytes accessed | tf_op | source)
XLA Modules:
  0.0 760.1 jit_solution(1291417502378739657)
XLA Ops:
  8.1 11.0 %all_gather.24 = bf16[1,128,2304]{2,1,0:T(8,128)(2,1)S(1)} all-gather(bf16[1,128,1152]{2,1,0:T(8,128)(2,1)} %param.14), channel_id=1, replica_groups=mesh['context'=4,'dp'=4,'head'=2] {'head'}, dimensions={2}, use_global_device_ids=true | all-gather | bytes 884736 | tf_op jit(solution)/shard_map/all_gather | solution.py:119
  22.9 35.1 %copy.152 = bf16[2304,3,2048]{0,2,1:T(8,128)(2,1)} copy(bf16[2304,3,2048]{2,0,1:T(8,128)(2,1)} %param.16) | data formatting | bytes 56623104 | tf_op args[2]
  58.0 15.4 %fusion.134 = f32[128,3,16,128]{3,0,2,1:T(8,128)} fusion(bf16[3,16,128,2304]{3,2,1,0:T(8,128)(2,1)} %bitcast.472, bf16[1,128,2304]{2,1,0:T(8,128)(2,1)S(1)} %all_gather.24), kind=kOutput, calls=%fused_computation.216 | convolution fusion | flops 3623878656 | bytes 32047104 | tf_op jit(solution)/shard_map/dot_general | solution.py:125
  73.4 2.2 multiply_reduce_fusion.3
  75.6 2.3 slice.78
  78.3 2.8 fusion.118
  81.2 2.1 fusion.164
  96.2 2.1 convolution_bitcast_fusion.2
  99.8 3.2 bitcast_subtract_fusion
  107.0 12.9 %while.51 = (s32[]{:T(128)}, f32[16,128,128]{2,1,0:T(8,128)}, f32[16,128,128]{2,1,0:T(8,128)}, f32[2,16,128,128]{3,2,1,0:T(8,128)}, f32[2,16,128,128]{3,2,1,0:T(8,128)}, /*index=5*/s32[]{:T(128)}, s32[]{:T(128)}) while((s32[]{:T(128)}, f32[16,128,128]{2,1,0:T(8,128)}, f32[16,128,128]{2,1,0:T(8,128)}, ...), condition=%wide.region_3.4_spmd.clone, body=%wide.region_2.0_spmd.clone.sunk | while | flops 403177472 | bytes 24118416 | solution.py:112
  108.9 2.9 convolution_add_fusion.38
  115.4 2.9 convolution_add_fusion.38
  119.9 2.2 convert_element_type.153
  122.1 4.5 collective-permute-start
  126.6 2.2 convolution_multiply_fusion
  132.9 2.0 fusion.87
  134.9 8.4 %all_gather.25 = bf16[1,128,2304]{2,1,0:T(8,128)(2,1)} all-gather(bf16[1,128,1152]{2,1,0:T(8,128)(2,1)S(1)} %copy-done.97), channel_id=1, replica_groups=mesh['context'=4,'dp'=4,'head'=2] {'head'}, dimensions={2}, use_global_device_ids=true | all-gather | bytes 884736 | tf_op jit(solution)/shard_map/all_gather | solution.py:141
  143.2 13.1 %copy.257 = bf16[2048,2304]{1,0:T(8,128)(2,1)} copy(bf16[2048,2304]{0,1:T(8,128)(2,1)} %bitcast.482) | data formatting | bytes 18874368 | tf_op jit(solution)/shard_map/dot_general | solution.py:142
  156.4 5.8 fusion.136
  166.6 2.2 fusion.200
  170.1 2.3 fusion.77
  172.4 5.4 collective-permute-start.1
  177.7 2.4 copy.162
  187.7 4.4 collective-permute-start.2
  193.7 3.5 collective-permute-done.4
  201.7 9.2 %while.49 = (s32[]{:T(128)}, f32[16,128,128]{2,1,0:T(8,128)S(1)}, bf16[2,16,64,128]{3,2,0,1:T(8,128)(2,1)}, f32[2,16,128,128]{3,2,1,0:T(8,128)}, f32[2,16,128,12...) while((s32[]{:T(128)}, f32[16,128,128]{2,1,0:T(8,128)S(1)}, ...), condition=%wide.region_6.7_spmd, body=%wide.region_5.6_spmd.sunk | while | flops 302383104 | bytes 36178636 | solution.py:96
  217.5 23.3 %while.50 = (s32[]{:T(128)}, f32[16,128,128]{2,1,0:T(8,128)S(1)}, f32[2,16,64,128]{3,2,0,1:T(8,128)}, f32[2,16,64,128]{3,2,1,0:T(8,128)}, f32[2,16,128,128]{2,3,...) while((s32[]{:T(128)}, f32[16,128,128]{2,1,0:T(8,128)S(1)}, ...), condition=%wide.region_9.10_spmd, body=%wide.region_8.9_spmd.sunk | while | flops 604241920 | bytes 56627016 | solution.py:96
  217.5 3.6 fusion.360
  224.9 2.4 fusion.359
  229.1 3.5 fusion.360
  236.4 2.4 fusion.359
  240.8 2.7 fusion.105
  245.3 2.2 fusion.72
  272.2 2.7 fusion.172
  274.9 2.0 fusion.171
  277.0 2.3 fusion.107
  280.5 2.6 fusion.166
  283.1 2.3 fusion.195
  285.4 2.0 fusion.51
  287.4 3.0 copy.207
  290.5 4.5 fusion.66
  299.5 2.9 fusion.151
  303.5 3.8 fusion.98
  314.7 3.3 concatenate.7
  318.7 2.4 fusion.90
  325.8 1.9 copy.212
  332.9 11.5 %fusion.57 = f32[128,2304]{1,0:T(8,128)S(1)} fusion(bf16[2304,6144]{0,1:T(8,128)(2,1)} %bitcast.473, bf16[128,2048]{0,1:T(8,128)(2,1)S(1)} %copy-done.93, bf16[128,2048]{0,1:T(8,128)(2,1)S(1)} %get-tuple-element.464, bf16[128,2048]{0,1:T(8,128)(2,1)S(1)} %get-tuple-element.463), kind=kOutput, calls=%fused_computation.83 | convolution fusion | flops 3628597248 | bytes 31064064 | tf_op jit(solution)/shard_map/tc,dc->td/dot_general | solution.py:215
  346.1 7.1 convolution_convert_fusion.1
  354.3 175.0 %all-reduce.8.cloned.1.call-done = bf16[4656,128]{0,1:T(8,128)(2,1)} async-done(((bf16[4656,128]{0,1:T(8,128)(2,1)}), bf16[4656,128]{0,1:T(8,128)(2,1)}) %all-reduce.8.cloned.1.call-update) | async-done | bytes 1191952 | tf_op jit(solution)/shard_map/psum | solution.py:201
  529.4 2.2 slice.90
  531.6 5.1 convolution_convert_fusion.6
  538.5 4.9 convolution_convert_fusion.5
  543.5 4.9 convolution_convert_fusion.4
  548.5 21.4 %all-gather.22.cloned.1.call-done = bf16[1,512,2304]{2,1,0:T(8,128)(2,1)} async-done(((bf16[1,128,2304]{2,1,0:T(8,128)(2,1)}), bf16[1,512,2304]{2,1,0:T(8,128)(2,1)}) %all-gather.22.cloned.1.call-update) | async-done | bytes 2359312 | tf_op jit(solution)/shard_map/all_gather | solution.py:169
  569.9 47.1 %all-gather.12.cloned.1.call-done = bf16[512,2048]{0,1:T(8,128)(2,1)} async-done(((bf16[128,2048]{0,1:T(8,128)(2,1)}), bf16[512,2048]{0,1:T(8,128)(2,1)}) %all-gather.12.cloned.1.call-update) | async-done | bytes 2097168 | tf_op jit(solution)/shard_map/all_gather | solution.py:173
  616.9 5.6 convolution_convert_fusion.3
  629.8 1.9 copy.264
  631.7 1.8 copy.262
  633.5 2.7 copy.223
  636.2 9.6 %reduce-scatter.11.cloned.1.call-done = bf16[144,2048]{1,0:T(8,128)(2,1)} async-done(((bf16[576,2048]{1,0:T(8,128)(2,1)}), bf16[144,2048]{1,0:T(8,128)(2,1)}) %reduce-scatter.11.cloned.1.call-update) | async-done | bytes 589840 | tf_op jit(solution)/shard_map/reduce_scatter | solution.py:175
  645.8 35.2 %reduce-scatter.13.cloned.1.call-done = bf16[144,2048]{1,0:T(8,128)(2,1)} async-done(((bf16[576,2048]{1,0:T(8,128)(2,1)}), bf16[144,2048]{1,0:T(8,128)(2,1)}) %reduce-scatter.13.cloned.1.call-update) | async-done | bytes 589840 | tf_op jit(solution)/shard_map/reduce_scatter | solution.py:175
  681.1 35.4 %reduce-scatter.15.cloned.1.call-done = bf16[144,2048]{1,0:T(8,128)(2,1)} async-done(((bf16[576,2048]{1,0:T(8,128)(2,1)}), bf16[144,2048]{1,0:T(8,128)(2,1)}) %reduce-scatter.15.cloned.1.call-update) | async-done | bytes 589840 | tf_op jit(solution)/shard_map/reduce_scatter | solution.py:175
  716.4 2.8 pad_maximum_fusion
  719.3 33.1 %reduce-scatter.17.cloned.1.call-done = bf16[144,2048]{1,0:T(8,128)(2,1)} async-done(((bf16[576,2048]{1,0:T(8,128)(2,1)}), bf16[144,2048]{1,0:T(8,128)(2,1)}) %reduce-scatter.17.cloned.1.call-update) | async-done | bytes 589840 | tf_op jit(solution)/shard_map/reduce_scatter | solution.py:175
  (412 shorter events, 142.0 us)
Async XLA Ops:
  8.0 11.2 %copy-start = (bf16[2304,128]{1,0:T(8,128)(2,1)S(1)}, bf16[2304,128]{1,0:T(8,128)(2,1)}, u32[]{:S(2)}) copy-start(bf16[2304,128]{1,0:T(8,128)(2,1)} %param.18) | copy-start | bytes 1769476
  8.0 11.5 %copy-start.95 = (bf16[128,2048]{1,0:T(8,128)(2,1)S(1)}, bf16[128,2048]{1,0:T(8,128)(2,1)}, u32[]{:S(2)}) copy-start(bf16[128,2048]{1,0:T(8,128)(2,1)} %param.19) | copy-start | bytes 1572868
  8.0 11.5 %copy-start.103 = (f32[2048]{0:T(1024)S(1)}, f32[2048]{0:T(1024)}, u32[]{:S(2)}) copy-start(f32[2048]{0:T(1024)} %param.21) | copy-start | bytes 24580
  8.0 521.3 %all-reduce.8.cloned.1.call-start = ((), (), s32[]{:S(2)}) async-start(), calls=%async_computation.11 | async-start | bytes 2424832 | tf_op jit(solution)/shard_map/psum | solution.py:201
  19.1 294.2 %copy-start.37 = (bf16[1,128,2304]{2,1,0:T(8,128)(2,1)}, bf16[1,128,2304]{2,1,0:T(8,128)(2,1)S(1)}, u32[]{:S(2)}) copy-start(bf16[1,128,2304]{2,1,0:T(8,128)(2,1)S(1)} %all_gather.24) | copy-start | bytes 1769476
  73.4 4.5 copy-start.98
  81.2 45.5 %copy-start.3 = (f32[128,16,128]{2,0,1:T(8,128)}, f32[128,16,128]{2,0,1:T(8,128)S(1)}, u32[]{:S(2)}) copy-start(f32[128,16,128]{2,0,1:T(8,128)S(1)} %get-tuple-element.459) | copy-start | bytes 3145732
  91.3 3.2 copy-start.27
  92.6 7.2 copy-start.46
  94.5 5.4 copy-start.41
  108.9 2.9 copy-start.5
  115.4 2.9 copy-start.5
  119.9 6.7 copy-start.33
  122.1 47.9 %collective-permute-start = (bf16[16,128,128]{2,1,0:T(8,128)(2,1)}, bf16[16,128,128]{2,1,0:T(8,128)(2,1)}, u32[]{:S(2)}, u32[]{:S(2)}) collective-permute-start(bf16[16,128,128]{2,1,0:T(8,128)(2,1)} %convert_element_type.153), channel_id=1, source_target_pairs={{0,8},{8,16},{16,24},{1,9},{9,17},{17,25},{2,10},{10,18},{18,26},{... | collective-permute-start | bytes 1572872 | tf_op jit(solution)/shard_map/ppermute | solution.py:16
  130.2 32.1 %copy-start.72 = (f32[16,2,64,128]{3,2,1,0:T(8,128)}, f32[16,2,64,128]{3,2,1,0:T(8,128)S(1)}, u32[]{:S(2)}) copy-start(f32[16,2,64,128]{3,2,1,0:T(8,128)S(1)} %convolution_subtract_fusion) | copy-start | bytes 3145732
  163.4 3.0 copy-start.7
  166.6 3.5 copy-start.6
  166.6 3.5 copy-start.10
  168.7 13.9 %collective-permute-start.3 = (bf16[16,128,128]{2,1,0:T(8,128)(2,1)}, bf16[16,128,128]{2,1,0:T(8,128)(2,1)}, u32[]{:S(2)}, u32[]{:S(2)}) collective-permute-start(bf16[16,128,128]{2,1,0:T(8,128)(2,1)} %get-tuple-element.474), channel_id=1, source_target_pairs={{8,0},{16,8},{24,16},{9,1},{17,9},{25,17},{10,2},{18,10},{26,18},{... | collective-permute-start | bytes 1572872 | tf_op jit(solution)/shard_map/ppermute | solution.py:16
  172.4 13.7 %collective-permute-start.1 = (bf16[16,128,128]{2,1,0:T(8,128)(2,1)}, bf16[16,128,128]{2,1,0:T(8,128)(2,1)}, u32[]{:S(2)}, u32[]{:S(2)}) collective-permute-start(bf16[16,128,128]{2,1,0:T(8,128)(2,1)} %fusion.77), channel_id=1, source_target_pairs={{0,8},{8,16},{16,24},{1,9},{9,17},{17,25},{2,10},{10,18},{18,26},{... | collective-permute-start | bytes 1572872 | tf_op jit(solution)/shard_map/ppermute | solution.py:16
  177.7 4.9 copy-start.63
  180.1 6.0 copy-start.11
  184.4 7.7 %copy-start.39 = (f32[16,2,64,128]{3,2,1,0:T(8,128)S(1)}, f32[16,2,64,128]{3,2,1,0:T(8,128)}, u32[]{:S(2)}) copy-start(f32[16,2,64,128]{3,2,1,0:T(8,128)} %copy-done.38) | copy-start | bytes 3145732
  184.4 7.7 %copy-start.44 = (f32[16,2,64,64]{3,2,1,0:T(8,128)S(1)}, f32[16,2,64,64]{3,2,1,0:T(8,128)}, u32[]{:S(2)}) copy-start(f32[16,2,64,64]{3,2,1,0:T(8,128)} %copy-done.43) | copy-start | bytes 1572868
  184.4 12.8 %collective-permute-start.4 = (bf16[16,128,128]{2,1,0:T(8,128)(2,1)S(1)}, bf16[16,128,128]{2,1,0:T(8,128)(2,1)S(1)}, u32[]{:S(2)}, u32[]{:S(2)}) collective-permute-start(bf16[16,128,128]{2,1,0:T(8,128)(2,1)S(1)} %fusion.79), channel_id=1, source_target_pairs={{8,0},{16,8},{24,16},{9,1},{17,9},{25,17},{10,2},{18,10},{26,18},{... | collective-permute-start | bytes 1572872 | tf_op jit(solution)/shard_map/ppermute | solution.py:16
  187.7 12.4 %collective-permute-start.2 = (bf16[16,128,128]{2,1,0:T(8,128)(2,1)S(1)}, bf16[16,128,128]{2,1,0:T(8,128)(2,1)S(1)}, u32[]{:S(2)}, u32[]{:S(2)}) collective-permute-start(bf16[16,128,128]{2,1,0:T(8,128)(2,1)S(1)} %fusion.78), channel_id=1, source_target_pairs={{0,8},{8,16},{16,24},{1,9},{9,17},{17,25},{2,10},{10,18},{18,26},{... | collective-permute-start | bytes 1572872 | tf_op jit(solution)/shard_map/ppermute | solution.py:16
  198.8 12.2 %collective-permute-start.5 = (bf16[16,128,128]{2,1,0:T(8,128)(2,1)}, bf16[16,128,128]{2,1,0:T(8,128)(2,1)}, u32[]{:S(2)}, u32[]{:S(2)}) collective-permute-start(bf16[16,128,128]{2,1,0:T(8,128)(2,1)} %fusion.80), channel_id=1, source_target_pairs={{8,0},{16,8},{24,16},{9,1},{17,9},{25,17},{10,2},{18,10},{26,18},{... | collective-permute-start | bytes 1572872 | tf_op jit(solution)/shard_map/ppermute | solution.py:16
  203.3 2.4 copy-start.2
  203.3 2.4 copy-start.9
  207.9 2.4 copy-start.2
  207.9 2.4 copy-start.9
  217.5 3.6 copy-start.26
  222.8 4.5 copy-start.50
  229.1 3.5 copy-start.26
  234.3 4.5 copy-start.50
  240.8 2.7 copy-start.45
  240.8 2.7 copy-start.54
  258.3 12.3 %copy-start.74 = (f32[16,2,64,64]{3,2,1,0:T(8,128)}, f32[16,2,64,64]{3,2,1,0:T(8,128)S(1)}, u32[]{:S(2)}) copy-start(f32[16,2,64,64]{3,2,1,0:T(8,128)S(1)} %convolution_add_fusion.7) | copy-start | bytes 1572868
  290.5 4.5 copy-start.14
  290.5 4.5 copy-start.23
  290.5 4.5 copy-start.75
  290.5 4.5 copy-start.90
  290.5 4.5 copy-start.91
  299.5 3.9 copy-start.29
  299.5 3.9 copy-start.55
  299.5 3.9 copy-start.77
  314.7 4.0 copy-start.78
  314.7 4.0 copy-start.79
  318.0 213.6 %all-gather.14.cloned.1.call-start = ((), (), s32[]{:S(2)}) async-start(), calls=%async_computation.13 | async-start | bytes 2949120 | tf_op jit(solution)/shard_map/all_gather | solution.py:169
  318.6 213.0 %all-gather.16.cloned.1.call-start = ((), (), s32[]{:S(2)}) async-start(), calls=%async_computation.14 | async-start | bytes 2621440 | tf_op jit(solution)/shard_map/all_gather | solution.py:173
  318.7 2.5 copy-start.30
  318.7 2.5 copy-start.62
  329.3 207.6 %all-gather.18.cloned.1.call-start = ((), (), s32[]{:S(2)}) async-start(), calls=%async_computation.15 | async-start | bytes 2621440 | tf_op jit(solution)/shard_map/all_gather | solution.py:173
  329.9 213.6 %all-gather.20.cloned.1.call-start = ((), (), s32[]{:S(2)}) async-start(), calls=%async_computation.16 | async-start | bytes 2621440 | tf_op jit(solution)/shard_map/all_gather | solution.py:173
  330.6 239.2 %all-gather.22.cloned.1.call-start = ((), (), s32[]{:S(2)}) async-start(), calls=%async_computation.17 | async-start | bytes 2949120 | tf_op jit(solution)/shard_map/all_gather | solution.py:169
  331.4 285.6 %all-gather.12.cloned.1.call-start = ((), (), s32[]{:S(2)}) async-start(), calls=%async_computation.9 | async-start | bytes 2621440 | tf_op jit(solution)/shard_map/all_gather | solution.py:173
  332.5 297.3 %reduce-scatter.21.cloned.1.call-start = ((), (), s32[]{:S(2)}) async-start(), calls=%async_computation.19 | async-start | bytes 884736
  332.9 11.5 %copy-start.99 = (bf16[2304,16]{0,1:T(8,128)(2,1)S(1)}, bf16[2304,16]{0,1:T(8,128)(2,1)}, u32[]{:S(2)}) copy-start(bf16[2304,16]{0,1:T(8,128)(2,1)} %param.20) | copy-start | bytes 221188
  345.8 285.9 %reduce-scatter.19.cloned.1.call-start = ((), (), s32[]{:S(2)}) async-start(), calls=%async_computation.18 | async-start | bytes 884736
  354.3 279.3 %all-reduce.10.cloned.1.call-start = ((), (), s32[]{:S(2)}) async-start(), calls=%async_computation.12 | async-start | bytes 2359296 | tf_op jit(solution)/shard_map/psum | solution.py:208
  531.5 114.3 %reduce-scatter.11.cloned.1.call-start = ((), (), s32[]{:S(2)}) async-start(), calls=%async_computation.6 | async-start | bytes 2949120 | tf_op jit(solution)/shard_map/reduce_scatter | solution.py:175
  536.8 144.3 %reduce-scatter.13.cloned.1.call-start = ((), (), s32[]{:S(2)}) async-start(), calls=%async_computation.7 | async-start | bytes 2949120 | tf_op jit(solution)/shard_map/reduce_scatter | solution.py:175
  543.4 173.0 %reduce-scatter.15.cloned.1.call-start = ((), (), s32[]{:S(2)}) async-start(), calls=%async_computation.8 | async-start | bytes 2949120 | tf_op jit(solution)/shard_map/reduce_scatter | solution.py:175
  548.4 203.9 %reduce-scatter.17.cloned.1.call-start = ((), (), s32[]{:S(2)}) async-start(), calls=%async_computation.10 | async-start | bytes 2949120 | tf_op jit(solution)/shard_map/reduce_scatter | solution.py:175
  (73 other events, 113.2 us)
Sparse Core Ops, SparseCore 0:
  318.1 211.1 all-reduce.7
  531.6 14.9 reduce-scatter.20
  549.5 15.3 reduce-scatter.18
  567.6 42.9 all-reduce.9
  612.9 32.8 reduce-scatter.10
  648.2 32.8 reduce-scatter.12
  683.6 32.8 reduce-scatter.14
  719.5 32.8 reduce-scatter.16
Sparse Core Ops, SparseCore 1:
  320.6 54.9 all-gather.13
  377.1 46.4 all-gather.15
  425.0 45.9 all-gather.17
  472.5 47.0 all-gather.19
  521.1 48.7 all-gather.21
  572.0 44.9 all-gather.11

commit v2 on v1

v2 whole, which is shorter than its diff:
```python
import jax
import jax.numpy as jnp
from jax import lax
from jax.experimental import pallas as pl
from jax.experimental.pallas import tpu as pltpu
from jax.sharding import PartitionSpec as P

SPAN = 64


epsilon = 1e-06
highest = lax.Precision.HIGH


def shifted(value, axis, by):
    count = lax.axis_size(axis)
    pairs = [(i, i + by) for i in range(count) if 0 <= i + by < count]
    return lax.ppermute(value, axis, pairs)


def product(pattern, left, right):
    return jnp.einsum(pattern, left, right, precision=highest)


def halves(value):
    high = value.astype(jnp.bfloat16)
    return high, (value - high.astype(jnp.float32)).astype(jnp.bfloat16)


def multiply(left, right, left_dim, right_dim):
    def one(first, second):
        return lax.dot_general(
            first,
            second,
            (((left_dim,), (right_dim,)), ((), ())),
            preferred_element_type=jnp.float32,
        )

    left_high, left_low = halves(left)
    right_high, right_low = halves(right)
    return (one(left_high, right_low) + one(left_low, right_high)) + one(left_high, right_high)


@jax.custom_vjp
def mat_nn(left, right):
    return multiply(left, right, 1, 0)


@jax.custom_vjp
def mat_nt(left, right):
    return multiply(left, right, 1, 1)


@jax.custom_vjp
def mat_tn(left, right):
    return multiply(left, right, 0, 0)


def keep(function):
    return lambda left, right: (function(left, right), (left, right))


mat_nn.defvjp(
    keep(mat_nn), lambda kept, grad: (mat_nt(grad, kept[1]), mat_tn(kept[0], grad))
)
mat_nt.defvjp(
    keep(mat_nt), lambda kept, grad: (mat_nn(grad, kept[1]), mat_tn(grad, kept[0]))
)
mat_tn.defvjp(
    keep(mat_tn), lambda kept, grad: (mat_nt(kept[1], grad), mat_nn(kept[0], grad))
)


def identity_of(side):
    row_index = lax.broadcasted_iota(jnp.int32, (side, side), 0)
    col_index = lax.broadcasted_iota(jnp.int32, (side, side), 1)
    return (row_index == col_index).astype(jnp.float32)


@jax.custom_vjp
def unit_inverse(coupling):
    powers = -coupling
    inverse = identity_of(SPAN) + powers
    for section in range(1, (SPAN - 1).bit_length()):
        powers = mat_nn(powers, powers)
        inverse = inverse + mat_nn(inverse, powers)
    return inverse


def inverse_forward(coupling):
    inverse = unit_inverse(coupling)
    return inverse, inverse


def inverse_backward(inverse, grad):
    return (-mat_nt(mat_tn(inverse, grad), inverse),)


unit_inverse.defvjp(inverse_forward, inverse_backward)


def block_terms(query_raw, key_raw, value_rows, gate, beta_raw):
    def normalize(values):
        return values * lax.rsqrt(jnp.sum(values * values, axis=-1, keepdims=True) + epsilon)

    queries, key_rows = normalize(query_raw), normalize(key_raw)
    decays = -0.25 * lax.logistic(gate)
    betas = lax.logistic(beta_raw)
    row_index = lax.broadcasted_iota(jnp.int32, (SPAN, SPAN), 0)
    col_index = lax.broadcasted_iota(jnp.int32, (SPAN, SPAN), 1)
    strict = (row_index > col_index).astype(jnp.float32)
    lower_mask = (row_index >= col_index).astype(jnp.float32)
    wide_index = lax.broadcasted_iota(jnp.int32, decays.shape, 0)
    cumulative = mat_nn(lower_mask, decays)
    middle = lax.stop_gradient(
        jnp.sum(jnp.where(wide_index < SPAN // 2, decays, 0.0), axis=0, keepdims=True)
    )
    final_decay = jnp.sum(decays, axis=0, keepdims=True)
    grow = jnp.exp(cumulative - middle)
    start = jnp.exp(cumulative)
    key_fwd = grow * key_rows
    key_back = jnp.exp(middle - cumulative) * key_rows
    query_fwd = grow * queries
    key_start = start * key_rows
    query_start = start * queries
    key_end = jnp.exp(final_decay - cumulative) * key_rows
    coupling = betas * mat_nt(key_fwd, key_back) * strict
    inverse = unit_inverse(coupling)
    solved_values = mat_nn(inverse, betas * value_rows)
    solved_keys = mat_nn(inverse, betas * key_start)
    scores = mat_nt(query_fwd, key_back) * lower_mask
    query_eff = query_start - mat_nn(scores, solved_keys)
    local_out = mat_nn(scores, solved_values)
    transition = identity_of(gate.shape[1]) * jnp.exp(final_decay) - mat_tn(key_end, solved_keys)
    offset = mat_tn(key_end, solved_values)
    return query_eff, local_out, transition, offset


def run_blocks(pieces, state):
    emitted = []
    for piece in pieces:
        query_eff, local_out, transition, offset = block_terms(*piece)
        emitted.append(mat_nn(query_eff, state) + local_out)
        state = mat_nn(transition, state) + offset
    return emitted, state


def head_pieces(refs, part, width, head):
    columns = slice(part * width, (part + 1) * width)
    logits = refs[4][...]
    picked = lax.broadcasted_iota(jnp.int32, logits.shape, 1) == head
    beta_raw = jnp.sum(jnp.where(picked, logits, 0.0), axis=1, keepdims=True)
    pieces = []
    for block in range(logits.shape[0] // SPAN):
        rows = slice(block * SPAN, (block + 1) * SPAN)
        pieces.append(tuple(ref[rows, columns] for ref in refs[:4]) + (beta_raw[rows],))
    return pieces, columns, picked


def summary_kernel(*refs):
    grad_ref, linear_ref, offset_ref, own_ref = refs[5:]
    together, width = linear_ref.shape[0], linear_ref.shape[1]
    for part in range(together):
        head = pl.program_id(0) * together + part
        pieces, columns, picked = head_pieces(refs, part, width, head)
        terms = [block_terms(*piece) for piece in pieces]
        linear, total = terms[0][2], terms[0][3]
        for term in terms[1:]:
            linear = mat_nn(term[2], linear)
            total = mat_nn(term[2], total) + term[3]
        own = None
        for block in reversed(range(len(terms))):
            rows = slice(block * SPAN, (block + 1) * SPAN)
            local = mat_tn(terms[block][0], grad_ref[rows, columns])
            own = local if own is None else mat_tn(terms[block][2], own) + local
        linear_ref[part] = linear
        offset_ref[part] = total
        own_ref[part] = own


def gradient_kernel(*refs):
    grad_ref, state_ref, after_ref = refs[5:8]
    mixed_ref, query_ref, key_ref, value_ref, gate_ref, bias_ref, logit_ref = refs[8:]
    together, width = state_ref.shape[0], state_ref.shape[1]

    @pl.when(pl.program_id(0) == 0)
    def clear():
        logit_ref[...] = jnp.zeros_like(logit_ref)

    for part in range(together):
        head = pl.program_id(0) * together + part
        pieces, columns, picked = head_pieces(refs, part, width, head)
        state = state_ref[part]
        outs, pull = jax.vjp(lambda given: run_blocks(given, state), pieces)
        count = len(pieces)
        grads = [grad_ref[slice(n * SPAN, (n + 1) * SPAN), columns] for n in range(count)]
        (piece_grads,) = pull((grads, after_ref[part]))
        bias = jnp.zeros((1, width), jnp.float32)
        for block in range(count):
            rows = slice(block * SPAN, (block + 1) * SPAN)
            query_grad, key_grad, value_grad, gate_grad, beta_grad = piece_grads[block]
            mixed_ref[rows, columns] = outs[0][block].astype(jnp.bfloat16)
            query_ref[rows, columns] = query_grad.astype(jnp.bfloat16)
            key_ref[rows, columns] = key_grad.astype(jnp.bfloat16)
            value_ref[rows, columns] = value_grad.astype(jnp.bfloat16)
            gate_ref[rows, columns] = gate_grad.astype(jnp.bfloat16)
            bias = bias + jnp.sum(gate_grad, axis=0, keepdims=True)
            logit_ref[rows, :] += jnp.where(picked[rows], beta_grad, 0.0)
        bias_ref[:, columns] = bias


def head_calls(projected, gate_pre, beta_logit, mixed_grad, together=2):
    token_count, all_width = gate_pre.shape
    head_count = beta_logit.shape[1]
    width = all_width // head_count
    steps = head_count // together

    def column(shift):
        return pl.BlockSpec((token_count, together * width), lambda step: (0, step + shift * steps))

    whole = pl.BlockSpec((token_count, head_count), lambda step: (0, 0))
    states = pl.BlockSpec((together, width, width), lambda step: (step, 0, 0))
    state_shape = jax.ShapeDtypeStruct((head_count, width, width), jnp.float32)
    wide_shape = jax.ShapeDtypeStruct((token_count, all_width), jnp.bfloat16)
    common = [column(0), column(1), column(2), column(0), whole, column(0)]
    given = (projected, projected, projected, gate_pre, beta_logit, mixed_grad)
    params = pltpu.CompilerParams(vmem_limit_bytes=48 * 1024 * 1024)

    def summary():
        return pl.pallas_call(
            summary_kernel,
            grid=(steps,),
            in_specs=common,
            out_specs=[states] * 3,
            out_shape=[state_shape] * 3,
            compiler_params=params,
        )(*given)

    def gradient(state_in, state_grad):
        return pl.pallas_call(
            gradient_kernel,
            grid=(steps,),
            in_specs=common + [states, states],
            out_specs=[column(0)] * 5
            + [pl.BlockSpec((1, together * width), lambda step: (0, step)), whole],
            out_shape=[wide_shape] * 5
            + [
                jax.ShapeDtypeStruct((1, all_width), jnp.float32),
                jax.ShapeDtypeStruct((token_count, head_count), jnp.float32),
            ],
            compiler_params=params,
        )(*given, state_in, state_grad)

    return summary, gradient


def shards(
    inputs, output_grad, qkv_weight, out_weight, down_weight, up_weight, beta_weight, gate_bias
):
    gathered = lax.all_gather(inputs, "head", axis=2, tiled=True)[0]
    token_count, model_width = gathered.shape
    all_width = qkv_weight.shape[2]
    head_count = beta_weight.shape[1]
    head_width = all_width // head_count
    qkv_flat = qkv_weight.reshape(model_width, 3 * all_width)
    projected = jnp.dot(gathered, qkv_flat, preferred_element_type=jnp.float32)
    low_rank = jnp.dot(gathered, down_weight, preferred_element_type=jnp.float32).astype(
        jnp.bfloat16
    )
    gate_pre = jnp.dot(low_rank, up_weight, preferred_element_type=jnp.float32) + gate_bias
    beta_logit = jnp.dot(gathered, beta_weight, preferred_element_type=jnp.float32)
    empty = jnp.zeros((head_count, head_width, head_width), jnp.float32)
    grad_whole = lax.all_gather(output_grad, "head", axis=2, tiled=True)[0]
    mixed_grad = jnp.dot(grad_whole, out_weight, preferred_element_type=jnp.float32)
    summary, gradient = head_calls(projected, gate_pre, beta_logit, mixed_grad)
    shard_linear, shard_offset, own_grad = summary()
    linear_back = jnp.swapaxes(shard_linear, 1, 2)
    shard_count = lax.axis_size("context")
    shard_index = lax.axis_index("context")
    state_in, state_grad = empty, empty
    for step in range(shard_count - 1):
        leaving = shard_offset
        leaving_grad = own_grad
        if step:
            leaving = product("hcd,hde->hce", shard_linear, state_in) + leaving
            leaving_grad = product("hcd,hde->hce", linear_back, state_grad) + leaving_grad
        state_in = shifted(leaving.astype(jnp.bfloat16), "context", 1).astype(jnp.float32)
        state_grad = shifted(leaving_grad.astype(jnp.bfloat16), "context", -1).astype(jnp.float32)
    mixed, *proj_parts, gate_low, bias_term, logit_grad = gradient(state_in, state_grad)
    slab = model_width // shard_count

    def slab_of(member):
        whole = lax.all_gather(member, "context", axis=0, tiled=True)
        return lax.dynamic_slice_in_dim(whole, shard_index * slab, slab, axis=1)

    def weight_term(rows, columns):
        whole = lax.all_gather(columns, "context", axis=0, tiled=True)
        term = jnp.einsum("tr,tc->rc", rows, whole, preferred_element_type=jnp.float32)
        return lax.psum_scatter(
            term.astype(jnp.bfloat16), "dp", scatter_dimension=0, tiled=True
        )

    input_slab = slab_of(gathered)
    grad_slab = slab_of(grad_whole)
    out_grad = weight_term(grad_slab, mixed)
    out_part = jnp.einsum("tc,dc->td", mixed, out_weight, preferred_element_type=jnp.float32)
    layer_out = lax.psum_scatter(
        out_part.astype(jnp.bfloat16), "head", scatter_dimension=1, tiled=True
    )[None]
    qkv_grad = jnp.stack([weight_term(input_slab, part) for part in proj_parts], axis=1)
    logit_low = logit_grad.astype(jnp.bfloat16)
    low_grad = jnp.einsum(
        "tc,rc->tr", gate_low, up_weight, preferred_element_type=jnp.float32
    ).astype(jnp.bfloat16)
    up_term = jnp.einsum("tr,tc->rc", low_rank, gate_low, preferred_element_type=jnp.float32)
    beta_term = jnp.einsum("td,th->dh", gathered, logit_low, preferred_element_type=jnp.float32)
    bias_term = bias_term[0]
    down_term = jnp.einsum("td,tr->dr", gathered, low_grad, preferred_element_type=jnp.float32)
    small = [up_term, down_term, beta_term, bias_term]
    packed = jnp.concatenate([term.astype(jnp.bfloat16).reshape(-1, 128) for term in small], axis=0)
    packed = lax.psum(packed, ("context", "dp")).astype(jnp.float32)
    results, start = [], 0
    for term in small:
        count = term.size // 128
        results.append(packed[start : start + count].reshape(term.shape))
        start += count
    up_grad, down_grad, beta_grad, bias_grad = results
    down_grad = lax.psum(down_grad, "head")
    input_part = jnp.einsum(
        "tr,dr->td", low_grad, down_weight, preferred_element_type=jnp.float32
    )
    input_part = input_part + jnp.einsum(
        "th,dh->td", logit_low, beta_weight, preferred_element_type=jnp.float32
    )
    input_part = input_part + jnp.einsum(
        "tc,dc->td",
        jnp.concatenate(proj_parts, axis=1),
        qkv_flat,
        preferred_element_type=jnp.float32,
    )
    input_grad = lax.psum_scatter(
        input_part.astype(jnp.bfloat16), "head", scatter_dimension=1, tiled=True
    )[None]
    return (layer_out, input_grad, qkv_grad, out_grad, up_grad, down_grad, beta_grad, bias_grad)


def solution(mesh):
    return jax.shard_map(
        shards,
        mesh=mesh,
        in_specs=(
            P("dp", "context", "head"),
            P("dp", "context", "head"),
            P(None, None, "head"),
            P(None, "head"),
            P(),
            P(None, "head"),
            P(None, "head"),
            P("head"),
        ),
        out_specs=(
            P("dp", "context", "head"),
            P("dp", "context", "head"),
            P(("context", "dp"), None, "head"),
            P(("context", "dp"), "head"),
            P(None, "head"),
            P(),
            P(None, "head"),
            P("head"),
        ),
        check_vma=False,
    )
```

time: 768 us -> 723 us (0.941)
  Pallas kernels: 0 us -> 150 us
  matrix products: 184 us -> 64.6 us
  local copies, waits for them, and re-layouts: 132 us -> 56.5 us
  waiting for transfers between devices: 365 us -> 394 us
  other arithmetic: 22.7 us -> 4.2 us
    pallas_call x0 -> x2, Pallas kernels: none -> 150 us  [the longest x1 93.7 us: gradient(): pl.pallas_call(gradient_kernel, grid=(steps,), in_specs=common + [states,...]
    dot_general x78 -> x4, matrix products: 120 us -> 2.36 us  [product(): return jnp.einsum(pattern, left, right, precision=highest)]
    unnamed x192 -> x27, local copies, waits for them, and re-layouts: 65.9 us -> 46 us
    ppermute x6, waiting for transfers between devices: 5.3 us -> 24.7 us  [shifted(): return lax.ppermute(value, axis, pairs)]
    while x60 -> x0, local copies, waits for them, and re-layouts: 17.7 us -> none
    dot_general x1 -> x0, local copies, waits for them, and re-layouts: 13.1 us -> none  [shards(): jnp.dot(grad_whole, out_weight, preferred_element_type=jnp.float32)]
    another operation x7 -> x0, local copies, waits for them, and re-layouts: 10.4 us -> none
    psum x1, waiting for transfers between devices: 175 us -> 183 us  [shards(): packed = lax.psum(packed, ('context', 'dp')).astype(jnp.float32)]
  transfers between devices with their start and end apart: 20 -> 20, of which waited for: 10 -> 11; matrix products, arithmetic and copies ran while one was open for 16% -> 8% of each run, Pallas kernels for 0% -> 0%
where the time goes in v2:
time: 723 us; the launch traced here: 722 us
  waiting for transfers between devices  394 us (54%)
  Pallas kernels  150 us (21%)
  matrix products  64.6 us (9%)
  local copies, waits for them, and re-layouts  56.5 us (8%)
  blocking collectives  19.5 us (3%)
  starting transfers between devices  17.2 us (2%)
  between operations  16 us (2%)
    psum x1, waiting for transfers between devices, shards(): packed = lax.psum(packed, ('context', 'dp')).astype(jnp.float32)  183 us
    reduce_scatter x4, waiting for transfers between devices, weight_term(): lax.psum_scatter(term.astype(jnp.bfloat16), 'dp', scatter_dimension=0, ti...  115 us
    pallas_call x1, Pallas kernels, gradient(): pl.pallas_call(gradient_kernel, grid=(steps,), in_specs=common + [states,...  93.7 us
    pallas_call x1, Pallas kernels, summary(): pl.pallas_call(summary_kernel, grid=(steps,), in_specs=common, out_specs=...  56 us
    unnamed x27, local copies, waits for them, and re-layouts  46 us
    all_gather x4, waiting for transfers between devices, weight_term(): whole = lax.all_gather(columns, 'context', axis=0, tiled=True)  46 us
    ppermute x6, waiting for transfers between devices, shifted(): return lax.ppermute(value, axis, pairs)  24.7 us
    all_gather x2, waiting for transfers between devices, slab_of(): whole = lax.all_gather(member, 'context', axis=0, tiled=True)  22 us
  transfers between devices with their start and end apart: 20, of which 11 were waited for; matrix products, arithmetic and copies ran while one was open for 8% of the time, Pallas kernels for 0%

profile of v2, /device:TPU:0, one launch (start us, length us, event | category | flops | bytes accessed | tf_op | source)
XLA Modules:
  0.0 721.5 jit_solution(13362472471097524939)
XLA Ops:
  8.1 33.5 %copy.35 = bf16[2304,3,2048]{0,2,1:T(8,128)(2,1)} copy(bf16[2304,3,2048]{2,0,1:T(8,128)(2,1)} %param.10) | data formatting | bytes 56623104 | tf_op args[2]
  41.5 10.6 %all_gather.24 = bf16[1,128,2304]{2,1,0:T(8,128)(2,1)S(1)} all-gather(bf16[1,128,1152]{2,1,0:T(8,128)(2,1)S(1)} %copy-done.5), channel_id=1, replica_groups=mesh['context'=4,'dp'=4,'head'=2] {'head'}, dimensions={2}, use_global_device_ids=true | all-gather | bytes 884736 | tf_op jit(solution)/shard_map/all_gather | solution.py:260
  52.2 16.1 %fusion.26.refs_0_.refs_1_.refs_2_ = f32[128,6144]{1,0:T(8,128)} fusion(bf16[2304,6144]{0,1:T(8,128)(2,1)} %bitcast.69, bf16[1,128,2304]{2,1,0:T(8,128)(2,1)S(1)} %all_gather.24), kind=kOutput, calls=%fused_computation.43 | convolution fusion | flops 3623878656 | bytes 32047104 | tf_op jit(solution)/shard_map/dot_general | solution.py:266
  68.3 0.3 convolution_convert_fusion.9
  68.9 8.8 %all_gather.25 = bf16[1,128,2304]{2,1,0:T(8,128)(2,1)S(1)} all-gather(bf16[1,128,1152]{2,1,0:T(8,128)(2,1)S(1)} %copy-done.6), channel_id=1, replica_groups=mesh['context'=4,'dp'=4,'head'=2] {'head'}, dimensions={2}, use_global_device_ids=true | all-gather | bytes 884736 | tf_op jit(solution)/shard_map/all_gather | solution.py:273
  77.8 5.3 fusion.19.refs_5_
  83.4 56.0 %shard_map.143 = (f32[16,128,128]{2,1,0:T(8,128)S(1)}, f32[16,128,128]{2,1,0:T(8,128)S(1)}, f32[16,128,128]{2,1,0:T(8,128)S(1)}) custom-call(f32[128,6144]{1,0:T(8,128)} %fusion.26.refs_0_.refs_1_.refs_2_, f32[128,6144]{1,0:T(8,128)} %fusion.26.refs_0_.refs_1_.refs_2_, f32[128,6144]{1,0:T(8,128)} %fusion.26.refs_0_.refs_1_.refs_2_, ...), custom_call_target="tpu_custom_call" | custom-call | tf_op jit(solution)/shard_map/pallas_call | solution.py:230
  139.5 3.5 collective-permute-start
  143.1 1.3 collective-permute-start.3
  144.4 8.0 %collective-permute-done = bf16[16,128,128]{2,1,0:T(8,128)(2,1)S(1)} collective-permute-done((bf16[16,128,128]{2,1,0:T(8,128)(2,1)S(1)}, bf16[16,128,128]{2,1,0:T(8,128)(2,1)S(1)}, u32[]{:S(2)}, u32[]{:S(2)}) %collective-permute-start) | collective-permute-done | bytes 524320 | tf_op jit(solution)/shard_map/ppermute | solution.py:18
  152.4 0.5 fusion.10
  152.8 4.4 collective-permute-start.1
  157.3 0.7 fusion.12
  158.0 1.3 collective-permute-start.4
  159.3 6.5 collective-permute-done.1
  165.8 0.5 fusion.11
  166.3 4.4 collective-permute-start.2
  170.7 0.7 fusion.13
  171.4 1.5 collective-permute-start.5
  172.9 5.5 collective-permute-done.2
  178.5 4.8 collective-permute-done.5
  183.3 1.1 convert_element_type.88.refs_7_
  184.3 93.7 %shard_map.144 = (bf16[128,2048]{1,0:T(8,128)(2,1)}, bf16[128,2048]{1,0:T(8,128)(2,1)}, bf16[128,2048]{1,0:T(8,128)(2,1)}, bf16[128,2048]{1,0:T(8,128)(2,1)}, bf...) custom-call(f32[128,6144]{1,0:T(8,128)} %fusion.26.refs_0_.refs_1_.refs_2_, ...), custom_call_target="tpu_custom_call" | custom-call | tf_op jit(solution)/shard_map/pallas_call | solution.py:240
  278.0 0.3 convolution_convert_fusion.8
  278.3 0.3 convolution_convert_fusion.7
  279.1 0.4 fusion.2
  279.7 0.3 copy.40
  280.0 0.4 reshape.40
  280.7 1.9 concatenate.7
  282.7 0.5 all-gather.17.cloned.1.call-update
  283.3 0.5 all-gather.13.cloned.1.call-update
  283.9 0.5 all-gather.11.cloned.1.call-update
  284.5 0.7 all-gather.9.cloned.1.call-update
  285.2 0.7 all-gather.19.cloned.1.call-update
  285.9 0.7 all-gather.15.cloned.1.call-update
  286.7 7.2 %convolution_convert_fusion.1 = bf16[128,2304]{1,0:T(8,128)(2,1)S(1)} fusion(bf16[128,2048]{1,0:T(8,128)(2,1)} %get-tuple-element.21, bf16[2304,2048]{1,0:T(8,128)(2,1)} %param.11), kind=kOutput, calls=%fused_computation.4 | convolution fusion | flops 1208254464 | bytes 10551296 | tf_op jit(solution)/shard_map/tc,dc->td/dot_general | solution.py:306
  293.9 1.1 copy.52
  295.3 11.9 %fusion.4 = f32[128,2304]{1,0:T(8,128)S(1)} fusion(bf16[2304,6144]{0,1:T(8,128)(2,1)} %bitcast.70, bf16[128,2048]{1,0:T(8,128)(2,1)} %get-tuple-element.26, bf16[128,2048]{1,0:T(8,128)(2,1)} %get-tuple-element.25, bf16[128,2048]{1,0:T(8,128)(2,1)} %get-tuple-element.24), kind=kOutput, calls=%fused_computation.15 | convolution fusion | flops 3628597248 | bytes 31064064 | tf_op jit(solution)/shard_map/tc,dc->td/dot_general | solution.py:335
  307.2 0.3 fusion.38
  307.8 1.1 copy.54
  308.9 182.7 %all-reduce.3.cloned.1.call-done = bf16[4656,128]{0,1:T(8,128)(2,1)} async-done(((bf16[4656,128]{0,1:T(8,128)(2,1)}), bf16[4656,128]{0,1:T(8,128)(2,1)}) %all-reduce.3.cloned.1.call-update) | async-done | bytes 1191952 | tf_op jit(solution)/shard_map/psum | solution.py:321
  491.7 2.2 slice.17
  493.9 4.8 convolution_convert_fusion.4
  498.9 1.7 copy-done.9
  500.6 4.6 convolution_convert_fusion.5
  505.3 4.7 convolution_convert_fusion.6
  510.1 22.0 %all-gather.19.cloned.1.call-done = bf16[1,512,2304]{2,1,0:T(8,128)(2,1)} async-done(((bf16[1,128,2304]{2,1,0:T(8,128)(2,1)}), bf16[1,512,2304]{2,1,0:T(8,128)(2,1)}) %all-gather.19.cloned.1.call-update) | async-done | bytes 2359312 | tf_op jit(solution)/shard_map/all_gather | solution.py:293
  532.1 45.9 %all-gather.15.cloned.1.call-done = bf16[512,2048]{1,0:T(8,128)(2,1)} async-done(((bf16[128,2048]{1,0:T(8,128)(2,1)}), bf16[512,2048]{1,0:T(8,128)(2,1)}) %all-gather.15.cloned.1.call-update) | async-done | bytes 2097168 | tf_op jit(solution)/shard_map/all_gather | solution.py:297
  578.0 4.9 convolution_convert_fusion.3
  582.9 1.3 copy-done.3
  584.2 1.1 slice.16
  585.3 1.5 copy.44
  586.9 1.1 reshape.41
  588.1 0.3 reshape.42
  588.5 1.0 copy.48
  589.6 0.7 copy.46
  590.2 1.8 copy.53
  592.1 1.8 copy.55
  593.9 2.7 copy.47
  596.6 10.9 %reduce-scatter.15.cloned.1.call-done = bf16[144,2048]{1,0:T(8,128)(2,1)} async-done(((bf16[576,2048]{1,0:T(8,128)(2,1)}), bf16[144,2048]{1,0:T(8,128)(2,1)}) %reduce-scatter.15.cloned.1.call-update) | async-done | bytes 589840 | tf_op jit(solution)/shard_map/reduce_scatter | solution.py:299
  607.5 35.2 %reduce-scatter.13.cloned.1.call-done = bf16[144,2048]{1,0:T(8,128)(2,1)} async-done(((bf16[576,2048]{1,0:T(8,128)(2,1)}), bf16[144,2048]{1,0:T(8,128)(2,1)}) %reduce-scatter.13.cloned.1.call-update) | async-done | bytes 589840 | tf_op jit(solution)/shard_map/reduce_scatter | solution.py:299
  642.8 35.4 %reduce-scatter.11.cloned.1.call-done = bf16[144,2048]{1,0:T(8,128)(2,1)} async-done(((bf16[576,2048]{1,0:T(8,128)(2,1)}), bf16[144,2048]{1,0:T(8,128)(2,1)}) %reduce-scatter.11.cloned.1.call-update) | async-done | bytes 589840 | tf_op jit(solution)/shard_map/reduce_scatter | solution.py:299
  678.1 2.8 pad_maximum_fusion
  681.0 33.1 %reduce-scatter.17.cloned.1.call-done = bf16[144,2048]{1,0:T(8,128)(2,1)} async-done(((bf16[576,2048]{1,0:T(8,128)(2,1)}), bf16[144,2048]{1,0:T(8,128)(2,1)}) %reduce-scatter.17.cloned.1.call-update) | async-done | bytes 589840 | tf_op jit(solution)/shard_map/reduce_scatter | solution.py:299
  (64 shorter events, 3.3 us)
Async XLA Ops:
  8.0 60.3 %copy-start = (bf16[2304,128]{1,0:T(8,128)(2,1)S(1)}, bf16[2304,128]{1,0:T(8,128)(2,1)}, u32[]{:S(2)}) copy-start(bf16[2304,128]{1,0:T(8,128)(2,1)} %param.12) | copy-start | bytes 1769476
  8.0 33.5 %copy-start.5 = (bf16[1,128,1152]{2,1,0:T(8,128)(2,1)S(1)}, bf16[1,128,1152]{2,1,0:T(8,128)(2,1)}, u32[]{:S(2)}) copy-start(bf16[1,128,1152]{2,1,0:T(8,128)(2,1)} %param.8) | copy-start | bytes 884740
  8.0 483.6 %all-reduce.3.cloned.1.call-start = ((), (), s32[]{:S(2)}) async-start(), calls=%async_computation.14 | async-start | bytes 2424832 | tf_op jit(solution)/shard_map/psum | solution.py:321
  52.2 227.3 %copy-start.1 = (bf16[1,128,2304]{2,1,0:T(8,128)(2,1)}, bf16[1,128,2304]{2,1,0:T(8,128)(2,1)S(1)}, u32[]{:S(2)}) copy-start(bf16[1,128,2304]{2,1,0:T(8,128)(2,1)S(1)} %all_gather.24) | copy-start | bytes 1769476
  52.2 16.4 %copy-start.7 = (bf16[2304,16]{0,1:T(8,128)(2,1)S(1)}, bf16[2304,16]{0,1:T(8,128)(2,1)}, u32[]{:S(2)}) copy-start(bf16[2304,16]{0,1:T(8,128)(2,1)} %param.14) | copy-start | bytes 221188
  52.2 16.7 %copy-start.6 = (bf16[1,128,1152]{2,1,0:T(8,128)(2,1)S(1)}, bf16[1,128,1152]{2,1,0:T(8,128)(2,1)}, u32[]{:S(2)}) copy-start(bf16[1,128,1152]{2,1,0:T(8,128)(2,1)} %param.9) | copy-start | bytes 884740
  77.8 5.3 copy-start.2
  77.8 5.3 copy-start.4
  77.8 5.3 copy-start.8
  139.5 12.9 %collective-permute-start = (bf16[16,128,128]{2,1,0:T(8,128)(2,1)S(1)}, bf16[16,128,128]{2,1,0:T(8,128)(2,1)S(1)}, u32[]{:S(2)}, u32[]{:S(2)}) collective-permute-start(bf16[16,128,128]{2,1,0:T(8,128)(2,1)S(1)} %convert_element_type.81), channel_id=1, source_target_pairs={{0,8},{8,16},{16,24},{1,9},{9,17},{17,25},{2,10},{10,18},{18,26},{... | collective-permute-start | bytes 1572872 | tf_op jit(solution)/shard_map/ppermute | solution.py:18
  143.1 14.2 %collective-permute-start.3 = (bf16[16,128,128]{2,1,0:T(8,128)(2,1)S(1)}, bf16[16,128,128]{2,1,0:T(8,128)(2,1)S(1)}, u32[]{:S(2)}, u32[]{:S(2)}) collective-permute-start(bf16[16,128,128]{2,1,0:T(8,128)(2,1)S(1)} %convert_element_type.85), channel_id=1, source_target_pairs={{8,0},{16,8},{24,16},{9,1},{17,9},{25,17},{10,2},{18,10},{26,18},{... | collective-permute-start | bytes 1572872 | tf_op jit(solution)/shard_map/ppermute | solution.py:18
  152.8 13.0 %collective-permute-start.1 = (bf16[16,128,128]{2,1,0:T(8,128)(2,1)S(1)}, bf16[16,128,128]{2,1,0:T(8,128)(2,1)S(1)}, u32[]{:S(2)}, u32[]{:S(2)}) collective-permute-start(bf16[16,128,128]{2,1,0:T(8,128)(2,1)S(1)} %fusion.10), channel_id=1, source_target_pairs={{0,8},{8,16},{16,24},{1,9},{9,17},{17,25},{2,10},{10,18},{18,26},{... | collective-permute-start | bytes 1572872 | tf_op jit(solution)/shard_map/ppermute | solution.py:18
  158.0 12.7 %collective-permute-start.4 = (bf16[16,128,128]{2,1,0:T(8,128)(2,1)S(1)}, bf16[16,128,128]{2,1,0:T(8,128)(2,1)S(1)}, u32[]{:S(2)}, u32[]{:S(2)}) collective-permute-start(bf16[16,128,128]{2,1,0:T(8,128)(2,1)S(1)} %fusion.12), channel_id=1, source_target_pairs={{8,0},{16,8},{24,16},{9,1},{17,9},{25,17},{10,2},{18,10},{26,18},{... | collective-permute-start | bytes 1572872 | tf_op jit(solution)/shard_map/ppermute | solution.py:18
  166.3 12.1 %collective-permute-start.2 = (bf16[16,128,128]{2,1,0:T(8,128)(2,1)S(1)}, bf16[16,128,128]{2,1,0:T(8,128)(2,1)S(1)}, u32[]{:S(2)}, u32[]{:S(2)}) collective-permute-start(bf16[16,128,128]{2,1,0:T(8,128)(2,1)S(1)} %fusion.11), channel_id=1, source_target_pairs={{0,8},{8,16},{16,24},{1,9},{9,17},{17,25},{2,10},{10,18},{18,26},{... | collective-permute-start | bytes 1572872 | tf_op jit(solution)/shard_map/ppermute | solution.py:18
  171.4 11.8 %collective-permute-start.5 = (bf16[16,128,128]{2,1,0:T(8,128)(2,1)S(1)}, bf16[16,128,128]{2,1,0:T(8,128)(2,1)S(1)}, u32[]{:S(2)}, u32[]{:S(2)}) collective-permute-start(bf16[16,128,128]{2,1,0:T(8,128)(2,1)S(1)} %fusion.13), channel_id=1, source_target_pairs={{8,0},{16,8},{24,16},{9,1},{17,9},{25,17},{10,2},{18,10},{26,18},{... | collective-permute-start | bytes 1572872 | tf_op jit(solution)/shard_map/ppermute | solution.py:18
  282.7 211.3 %all-gather.17.cloned.1.call-start = ((), (), s32[]{:S(2)}) async-start(), calls=%async_computation.16 | async-start | bytes 2949120 | tf_op jit(solution)/shard_map/all_gather | solution.py:293
  283.2 210.7 %all-gather.13.cloned.1.call-start = ((), (), s32[]{:S(2)}) async-start(), calls=%async_computation.10 | async-start | bytes 2621440 | tf_op jit(solution)/shard_map/all_gather | solution.py:297
  283.8 215.1 %all-gather.11.cloned.1.call-start = ((), (), s32[]{:S(2)}) async-start(), calls=%async_computation.8 | async-start | bytes 2621440 | tf_op jit(solution)/shard_map/all_gather | solution.py:297
  284.4 220.9 %all-gather.9.cloned.1.call-start = ((), (), s32[]{:S(2)}) async-start(), calls=%async_computation.6 | async-start | bytes 2621440 | tf_op jit(solution)/shard_map/all_gather | solution.py:297
  285.1 247.0 %all-gather.19.cloned.1.call-start = ((), (), s32[]{:S(2)}) async-start(), calls=%async_computation.17 | async-start | bytes 2949120 | tf_op jit(solution)/shard_map/all_gather | solution.py:293
  285.9 292.1 %all-gather.15.cloned.1.call-start = ((), (), s32[]{:S(2)}) async-start(), calls=%async_computation.12 | async-start | bytes 2621440 | tf_op jit(solution)/shard_map/all_gather | solution.py:297
  286.6 303.6 %reduce-scatter.19.cloned.1.call-start = ((), (), s32[]{:S(2)}) async-start(), calls=%async_computation.18 | async-start | bytes 884736
  295.0 297.0 %reduce-scatter.21.cloned.1.call-start = ((), (), s32[]{:S(2)}) async-start(), calls=%async_computation.19 | async-start | bytes 884736
  308.9 285.1 %all-reduce.5.cloned.1.call-start = ((), (), s32[]{:S(2)}) async-start(), calls=%async_computation.15 | async-start | bytes 2359296 | tf_op jit(solution)/shard_map/psum | solution.py:328
  493.8 113.7 %reduce-scatter.15.cloned.1.call-start = ((), (), s32[]{:S(2)}) async-start(), calls=%async_computation.11 | async-start | bytes 2949120 | tf_op jit(solution)/shard_map/reduce_scatter | solution.py:299
  498.8 1.8 copy-start.9
  498.8 143.9 %reduce-scatter.13.cloned.1.call-start = ((), (), s32[]{:S(2)}) async-start(), calls=%async_computation.9 | async-start | bytes 2949120 | tf_op jit(solution)/shard_map/reduce_scatter | solution.py:299
  505.3 172.9 %reduce-scatter.11.cloned.1.call-start = ((), (), s32[]{:S(2)}) async-start(), calls=%async_computation.7 | async-start | bytes 2949120 | tf_op jit(solution)/shard_map/reduce_scatter | solution.py:299
  510.1 204.0 %reduce-scatter.17.cloned.1.call-start = ((), (), s32[]{:S(2)}) async-start(), calls=%async_computation.13 | async-start | bytes 2949120 | tf_op jit(solution)/shard_map/reduce_scatter | solution.py:299
  582.9 1.3 copy-start.3
Sparse Core Ops, SparseCore 0:
  282.8 208.8 all-reduce.2
  493.9 14.9 reduce-scatter.18
  511.2 15.3 reduce-scatter.20
  529.3 42.9 all-reduce.4
  574.7 32.8 reduce-scatter.14
  609.9 32.8 reduce-scatter.12
  645.3 32.8 reduce-scatter.10
  681.2 32.8 reduce-scatter.16
Sparse Core Ops, SparseCore 1:
  285.3 52.8 all-gather.16
  339.6 46.1 all-gather.12
  387.2 46.0 all-gather.10
  434.8 47.0 all-gather.8
  483.5 48.5 all-gather.18
  533.7 44.3 all-gather.14
